TPU v7x, 256 devices: a whole 4x4x8 slice. The times are simulated.
256 devices in a mesh: pipe: 8 (over x, core), seq: 8 (over z), tensor: 4 (over y).
Axes of the slice: x: 4, y: 4, z: 8, core: 2. Of those that a mesh axis runs over, the one named last changes fastest.
Arguments:
- hidden: bfloat16 [8, 1024, 14336], P('pipe', 'seq', 'tensor'), may hold values from -6 to 6
- down_weight: bfloat16 [8, 14336, 8192], P('pipe', 'tensor', 'seq'), may hold values from -0.046875 to 0.046875
- resid: bfloat16 [1024, 8192], P('tensor', 'seq'), may hold values from -42 to 42
- target: bfloat16 [1024, 8192], P('tensor', 'seq'), may hold values from -6 to 6
- gain: float32 [8192], P('seq'), may hold values from 0.1 to 1.9
- query_left: float32 [8, 8192, 32], P('pipe', 'seq'), may hold values from -0.0625 to 0.0625
- query_right: bfloat16 [8, 14336, 32], P('pipe', 'tensor'), may hold values from -0.046875 to 0.046875
- query_core: float32 [8, 1024], P('pipe'), may hold values from -6 to 6
- eigen: float32 [8, 1024], P('pipe'), may hold values from 0.1 to 10
- lengths: int32 [32], replicated, may hold values from 1 to 256, 1024 in all
Outputs:
- scores: float32 [32], P(('seq', 'tensor'))
All inputs are finite; a program needn't handle non-finite values.
Results may differ from a plain program's by a relative error of at most 0.0006.
Values may be sent and summed in bfloat16 or wider, within the bound.
No kernel may reach another device: no remote copies, remote signals or barrier semaphores. Data moves between devices by JAX's collectives and lax.ppermute only.
A program may use at most 64 MiB of HBM per device.

v0:
```python
import jax
import jax.numpy as jnp
from jax import lax
from jax.sharding import PartitionSpec as P

D = 8192


def per_device(
    hidden, down_weight, resid, target, gain, query_left, query_right, query_core, eigen, lengths
):
    tensor_count = lax.axis_size("tensor")
    gathered = lax.all_gather(hidden[0], "seq", axis=0, tiled=True)
    total_rows = gathered.shape[0]
    block_rows = total_rows // tensor_count
    weight = down_weight[0]
    right_partial = jnp.dot(gathered, query_right[0], preferred_element_type=jnp.float32)
    partial_value = lax.psum_scatter(
        jnp.dot(gathered, weight, preferred_element_type=jnp.float32).astype(jnp.bfloat16),
        "tensor",
        scatter_dimension=0,
        tiled=True,
    ).astype(jnp.float32)
    summed = lax.psum(partial_value, "pipe")
    stream = resid.astype(jnp.float32) + summed
    weighted_target = gain[None, :] * target.astype(jnp.float32)
    square_sum, inner = lax.psum(
        (jnp.sum(stream * stream, axis=1), jnp.sum(weighted_target * stream, axis=1)), "seq"
    )
    root = jnp.sqrt(square_sum / D + 1e-05)
    grad_stream = (
        weighted_target / root[:, None] - stream * (inner / (D * root * root * root))[:, None]
    )
    left_proj = jnp.dot(grad_stream, query_left[0], precision=lax.Precision.HIGHEST)
    right_proj = lax.psum_scatter(right_partial, "tensor", scatter_dimension=0, tiled=True)
    rank_width = left_proj.shape[1]
    outer = (left_proj[:, :, None] * right_proj[:, None, :]).reshape(
        block_rows, rank_width * rank_width
    )
    ends = jnp.cumsum(lengths)
    starts = ends - lengths
    token = lax.axis_index("tensor") * block_rows + jnp.arange(block_rows, dtype=jnp.int32)
    member = ((token[None, :] >= starts[:, None]) & (token[None, :] < ends[:, None])).astype(
        jnp.float32
    )
    partial_cores = jnp.dot(member, outer, precision=lax.Precision.HIGHEST)
    cores = lax.psum_scatter(partial_cores, ("seq", "tensor"), scatter_dimension=0, tiled=True)
    scaled = cores / eigen[0][None, :]
    score_term = jnp.sum(query_core[0][None, :] * scaled, axis=1)
    self_term = jnp.sum(cores * scaled, axis=1)
    score_total, self_total = lax.psum((score_term, self_term), "pipe")
    return score_total / jnp.sqrt(self_total + 1e-06)


def solution(mesh):
    placed = (
        P("pipe", "seq", "tensor"),
        P("pipe", "tensor", "seq"),
        P("tensor", "seq"),
        P("tensor", "seq"),
        P("seq"),
        P("pipe", "seq", None),
        P("pipe", "tensor", None),
        P("pipe", None),
        P("pipe", None),
        P(),
    )
    return jax.shard_map(
        per_device, mesh=mesh, in_specs=placed, out_specs=P(("seq", "tensor")), check_vma=False
    )
```

profile of v0, /device:TPU:1, one launch (start us, length us, event | category | flops | bytes accessed | tf_op | source)
XLA Modules:
  0.0 375.0 jit_solution(16374362809391073880)
XLA Ops:
  6.5 0.7 all-gather.3.cloned.1.call-update
  7.3 0.0 reduce-scatter.3.cloned.1.call-start
  7.3 90.0 %all-gather.3.cloned.1.call-done = bf16[1,1024,3584]{2,1,0:T(8,128)(2,1)} async-done(((bf16[1,128,3584]{2,1,0:T(8,128)(2,1)}), bf16[1,1024,3584]{2,1,0:T(8,128)(2,1)}) %all-gather.3.cloned.1.call-update) | async-done | bytes 7340048 | tf_op jit(solution)/shard_map/all_gather | solution.py:13
  97.3 13.3 %fusion.5 = bf16[1024,1024]{1,0:T(8,128)(2,1)} fusion(bf16[1,3584,1024]{2,1,0:T(8,128)(2,1)} %param.11, bf16[1,1024,3584]{2,1,0:T(8,128)(2,1)} %all-gather.3.cloned.1.call-done), kind=kOutput, calls=%fused_computation.5 | convolution fusion | flops 7517241344 | bytes 16777216 | tf_op jit(solution)/shard_map/dot_general | solution.py:19
  110.6 0.0 reduce-scatter.3.cloned.1.call-update
  110.6 0.0 reduce-scatter.5.cloned.1.call-start
  110.7 0.1 copy.15
  110.8 0.1 reduce-window.8
  110.8 0.1 reduce.2
  111.0 6.0 %fusion.2 = f32[1024,32]{0,1:T(8,128)} fusion(bf16[1,1024,3584]{2,1,0:T(8,128)(2,1)} %all-gather.3.cloned.1.call-done, bf16[1,3584,32]{1,2,0:T(8,128)(2,1)S(1)} %copy-done), kind=kOutput, calls=%fused_computation.2 | convolution fusion | flops 234881024 | bytes 7700480 | tf_op jit(solution)/shard_map/dot_general | solution.py:17
  116.9 0.0 reduce-scatter.5.cloned.1.call-update
  117.0 0.0 all-reduce.6.cloned.1.call-start
  117.0 24.6 %reduce-scatter.3.cloned.1.call-done = bf16[256,1024]{1,0:T(8,128)(2,1)} async-done(((bf16[1024,1024]{1,0:T(8,128)(2,1)}), bf16[256,1024]{1,0:T(8,128)(2,1)}) %reduce-scatter.3.cloned.1.call-update) | async-done | bytes 524304 | tf_op jit(solution)/shard_map/reduce_scatter | solution.py:18
  141.7 50.4 %all-reduce.7 = f32[256,1024]{1,0:T(8,128)S(1)} all-reduce(bf16[256,1024]{1,0:T(8,128)(2,1)} %reduce-scatter.3.cloned.1.call-done), channel_id=1, replica_groups=mesh['pipe'=8,'seq'=8,'tensor'=4] {'pipe'}, use_global_device_ids=true, to_apply=%region_2.0 | all-reduce | flops 262144 | bytes 1572864 | tf_op jit(solution)/shard_map/psum | solution.py:24
  192.1 0.4 multiply_reduce_fusion.1
  192.5 13.7 %all-reduce.1 = (f32[256]{0:T(256)S(1)}, f32[256]{0:T(256)S(1)}) all-reduce(f32[256]{0:T(256)S(1)} %get-tuple-element.6, f32[256]{0:T(256)S(1)} %get-tuple-element.5), channel_id=1, replica_groups=mesh['pipe'=8,'seq'=8,'tensor'=4] {'seq'}, use_global_device_ids=true, to_apply=%region_6.0 | all-reduce | flops 512 | bytes 4096 | tf_op jit(solution)/shard_map/psum | solution.py:27
  206.2 1.2 fusion.10
  207.4 0.0 reduce-scatter.5.cloned.1.call-done
  207.5 0.9 broadcast_multiply_fusion
  208.3 1.3 fusion.19
  209.7 0.6 dynamic-slice
  210.3 137.4 %all-reduce.6.cloned.1.call-done = f32[32,1024]{1,0:T(8,128)} async-done(((f32[32,1024]{1,0:T(8,128)}), f32[32,1024]{1,0:T(8,128)}) %all-reduce.6.cloned.1.call-update) | async-done | bytes 131088
  347.7 2.0 multiply_reduce_fusion.2
  349.7 16.9 %all-reduce.2 = (f32[1]{0:T(128)}, f32[1]{0:T(128)}) all-reduce(f32[1]{0:T(128)} %bitcast.6, f32[1]{0:T(128)} %bitcast.7), channel_id=1, replica_groups=mesh['pipe'=8,'seq'=8,'tensor'=4] {'pipe'}, use_global_device_ids=true, to_apply=%region_10.11 | all-reduce | flops 2 | bytes 16 | tf_op jit(solution)/shard_map/psum | solution.py:51
  (23 shorter events, 0.1 us)
Async XLA Ops:
  6.5 104.4 %copy-start = (bf16[1,3584,32]{1,2,0:T(8,128)(2,1)S(1)}, bf16[1,3584,32]{1,2,0:T(8,128)(2,1)}, u32[]{:S(2)}) copy-start(bf16[1,3584,32]{1,2,0:T(8,128)(2,1)} %param.16) | copy-start | bytes 688132
  6.5 90.8 %all-gather.3.cloned.1.call-start = ((), (), s32[]{:S(2)}) async-start(), calls=%async_computation.4 | async-start | bytes 8257536 | tf_op jit(solution)/shard_map/all_gather | solution.py:13
  7.3 103.4 %copy-start.6 = (s32[32]{0:T(128)S(1)}, s32[32]{0:T(128)}, u32[]{:S(2)}) copy-start(s32[32]{0:T(128)} %param.19) | copy-start | bytes 388
  7.3 134.4 %reduce-scatter.3.cloned.1.call-start = ((), (), s32[]{:S(2)}) async-start(), calls=%async_computation.2 | async-start | bytes 2621440 | tf_op jit(solution)/shard_map/reduce_scatter | solution.py:18
  110.6 81.5 %copy-start.1 = (bf16[256,1024]{1,0:T(8,128)(2,1)S(1)}, bf16[256,1024]{1,0:T(8,128)(2,1)}, u32[]{:S(2)}) copy-start(bf16[256,1024]{1,0:T(8,128)(2,1)} %param.13) | copy-start | bytes 1572868
  110.6 81.5 %copy-start.2 = (bf16[256,1024]{1,0:T(8,128)(2,1)S(1)}, bf16[256,1024]{1,0:T(8,128)(2,1)}, u32[]{:S(2)}) copy-start(bf16[256,1024]{1,0:T(8,128)(2,1)} %param.12) | copy-start | bytes 1572868
  110.6 81.5 %copy-start.3 = (f32[1024]{0:T(1024)S(1)}, f32[1024]{0:T(1024)}, u32[]{:S(2)}) copy-start(f32[1024]{0:T(1024)} %param.14) | copy-start | bytes 12292
  110.6 95.6 %copy-start.7 = (f32[1,1024,32]{1,2,0:T(8,128)S(1)}, f32[1,1024,32]{1,2,0:T(8,128)}, u32[]{:S(2)}) copy-start(f32[1,1024,32]{1,2,0:T(8,128)} %param.15) | copy-start | bytes 393220
  110.6 96.9 %reduce-scatter.5.cloned.1.call-start = ((), (), s32[]{:S(2)}) async-start(), calls=%async_computation.3 | async-start | bytes 163840 | tf_op jit(solution)/shard_map/reduce_scatter | solution.py:35
  116.9 92.8 %copy-start.8 = (u32[256]{0:T(256)S(1)}, u32[256]{0:T(256)}, u32[]{:S(2)}) copy-start(u32[256]{0:T(256)} %constant.28) | copy-start | bytes 3076
  116.9 230.7 %copy-start.4 = (f32[1,1024]{1,0:T(1,128)S(1)}, f32[1,1024]{1,0:T(1,128)}, u32[]{:S(2)}) copy-start(f32[1,1024]{1,0:T(1,128)} %param.17) | copy-start | bytes 12292
  116.9 230.7 %copy-start.5 = (f32[1,1024]{1,0:T(1,128)S(1)}, f32[1,1024]{1,0:T(1,128)}, u32[]{:S(2)}) copy-start(f32[1,1024]{1,0:T(1,128)} %param.18) | copy-start | bytes 12292
  117.0 230.7 %all-reduce.6.cloned.1.call-start = ((), (), s32[]{:S(2)}) async-start(), calls=%async_computation.5 | async-start | bytes 262144
Sparse Core Ops, SparseCore 0:
  9.1 88.1 all-gather.2
  110.7 30.8 reduce-scatter.2
  144.3 20.4 reduce-scatter.4
  209.8 137.8 all-reduce.5
where the time goes:
time: 375 us
  waiting for transfers between devices  253 us (67%)
  blocking collectives  81 us (22%)
  matrix products  21.7 us (6%)
  between operations  15.1 us (4%)
    unnamed x5, waiting for transfers between devices  138 us
    all_gather x1, waiting for transfers between devices, per_device(): gathered = lax.all_gather(hidden[0], 'seq', axis=0, tiled=True)  90 us
    psum x1, blocking collectives, per_device(): summed = lax.psum(partial_value, 'pipe')  50.4 us
    reduce_scatter x1, waiting for transfers between devices, per_device(): lax.psum_scatter(jnp.dot(gathered, weight, preferred_element_type=jnp.flo...  24.6 us
    psum x1, blocking collectives, per_device(): score_total, self_total = lax.psum((score_term, self_term), 'pipe')  16.9 us
    psum x1, blocking collectives, per_device(): lax.psum((jnp.sum(stream * stream, axis=1), jnp.sum(weighted_target * str...  13.7 us
    dot_general x1, matrix products, per_device(): jnp.dot(gathered, weight, preferred_element_type=jnp.float32)  13.3 us
  transfers between devices with their start and end apart: 4, of which 3 were waited for; matrix products, arithmetic and copies ran while one was open for 2% of the time, Pallas kernels for 0%

commit v1 on v0

v1 whole, which is shorter than its diff:
```python
import jax
import jax.numpy as jnp
from jax import lax
from jax.sharding import PartitionSpec as P

D = 8192


def ring_blocks(x, axis):
    count = lax.axis_size(axis)
    half = x.shape[0] // 2
    up = [(i, (i + 1) % count) for i in range(count)]
    down = [(i, (i - 1) % count) for i in range(count)]
    up_low = down_low = x[:half]
    up_high = down_high = x[half:]
    groups = [[x]]
    for _ in range(count // 2 - 1):
        up_low = lax.ppermute(up_low, axis, up)
        down_high = lax.ppermute(down_high, axis, down)
        up_high = lax.ppermute(up_high, axis, up)
        down_low = lax.ppermute(down_low, axis, down)
        groups.append([up_low, up_high, down_low, down_high])
    up_low = lax.ppermute(up_low, axis, up)
    down_high = lax.ppermute(down_high, axis, down)
    groups.append([up_low, down_high])
    return groups


def ring_order(count):
    order = [0]
    for distance in range(1, count // 2):
        order += [-distance, distance]
    return order + [count // 2]


def per_device(
    hidden, down_weight, resid, target, gain, query_left, query_right, query_core, eigen, lengths
):
    layers = lax.axis_size("pipe")
    seqs = lax.axis_size("seq")
    tensors = lax.axis_size("tensor")
    layer = lax.axis_index("pipe")
    seq = lax.axis_index("seq")
    tensor = lax.axis_index("tensor")
    own = hidden[0]
    weight = down_weight[0]
    block_rows, width = own.shape[0], weight.shape[1]
    rank = query_left.shape[2]
    share = block_rows // (tensors * layers)
    strip = share * layers
    f32 = jnp.float32

    right_partial = jnp.dot(own, query_right[0], preferred_element_type=f32)
    right_parts = lax.all_to_all(right_partial.reshape(tensors, strip, rank), "tensor", 0, 0)
    right_proj = jnp.sum(right_parts, axis=0)

    own_left = jnp.transpose(query_left[0])
    left_all = lax.all_to_all(
        jnp.broadcast_to(own_left[None], (layers, rank, width)), "pipe", 0, 0
    ).reshape(layers * rank, width)

    local_blocks = seqs // tensors
    both = jnp.stack([resid, target]).reshape(2, local_blocks, tensors, layers, share, width)
    both = lax.dynamic_index_in_dim(both, layer, axis=3, keepdims=False)
    both = lax.all_to_all(jnp.transpose(both, (2, 0, 1, 3, 4)), "tensor", 0, 0)
    both = jnp.transpose(both, (1, 0, 2, 3, 4)).reshape(2, seqs * share, width)
    resid_rows, target_rows = both[0].astype(f32), both[1].astype(f32)
    weighted = gain[None, :] * target_rows

    groups = ring_blocks(own, "seq")
    products = []
    for pieces in groups:
        rows = pieces[0] if len(pieces) == 1 else jnp.concatenate(pieces, axis=0)
        products.append(jnp.dot(rows, weight, preferred_element_type=f32).astype(jnp.bfloat16))
    reduced = []
    for part in (products[:3], products[3:]):
        stacked = jnp.concatenate(part, axis=0)
        blocks = stacked.shape[0] // block_rows
        sent = jnp.transpose(
            stacked.reshape(blocks, tensors * layers, share, width), (1, 0, 2, 3)
        ).reshape(tensors * layers, blocks * share, width)
        got = lax.all_to_all(sent, ("tensor", "pipe"), 0, 0)
        reduced.append(jnp.sum(got.astype(f32), axis=0).reshape(blocks, share, width))
    summed = jnp.concatenate(reduced, axis=0)
    order = ring_order(seqs)
    by_offset = [order.index(o if o in order else o - seqs) for o in range(seqs)]
    summed = jnp.concatenate([summed[i : i + 1] for i in by_offset], axis=0)
    summed = jnp.roll(summed, seq, axis=0).reshape(seqs * share, width)
    stream = resid_rows + summed

    square_sum = jnp.sum(stream * stream, axis=1)
    inner = jnp.sum(weighted * stream, axis=1)
    projected = lax.dot_general(
        jnp.concatenate([weighted, stream], axis=0),
        left_all,
        (((1,), (1,)), ((), ())),
        precision=lax.Precision.HIGHEST,
        preferred_element_type=f32,
    ).reshape(2, seqs, share, layers, rank)
    projected = jnp.transpose(projected, (3, 1, 2, 0, 4)).reshape(
        layers, seqs, share, 2 * rank
    )
    stats = jnp.stack([square_sum, inner], axis=1).reshape(1, seqs, share, 2)
    packed = jnp.concatenate(
        [projected, jnp.broadcast_to(stats, (layers, seqs, share, 2))], axis=3
    ).reshape(layers * seqs, share, 2 * rank + 2)
    packed = lax.all_to_all(packed, ("pipe", "seq"), 0, 0)
    totals = jnp.sum(packed.reshape(layers, seqs, share, 2 * rank + 2), axis=1)
    totals = totals.reshape(strip, 2 * rank + 2)
    square_sum, inner = totals[:, 2 * rank], totals[:, 2 * rank + 1]
    root = jnp.sqrt(square_sum / D + 1e-05)
    left_proj = (
        totals[:, :rank] / root[:, None]
        - totals[:, rank : 2 * rank] * (inner / (D * root * root * root))[:, None]
    )

    outer = (left_proj[:, :, None] * right_proj[:, None, :]).reshape(strip, rank * rank)
    docs = lengths.shape[0]
    number = jnp.arange(docs, dtype=jnp.int32)
    starts = jnp.sum(jnp.where(number[None, :] < number[:, None], lengths[None, :], 0), axis=1)
    ends = starts + lengths
    token = seq * block_rows + tensor * strip + jnp.arange(strip, dtype=jnp.int32)
    member = ((token[None, :] >= starts[:, None]) & (token[None, :] < ends[:, None])).astype(f32)
    partial_cores = jnp.dot(member, outer, precision=lax.Precision.HIGHEST)
    cores = jnp.sum(lax.all_to_all(partial_cores, ("seq", "tensor"), 0, 0, tiled=True), axis=0)
    scaled = cores / eigen[0]
    terms = jnp.stack([jnp.sum(query_core[0] * scaled), jnp.sum(cores * scaled)])
    terms = jnp.sum(
        lax.all_to_all(jnp.broadcast_to(terms[None], (layers, 2)), "pipe", 0, 0, tiled=True), axis=0
    )
    return (terms[0] / jnp.sqrt(terms[1] + 1e-06)).reshape(1)


def solution(mesh):
    placed = (
        P("pipe", "seq", "tensor"),
        P("pipe", "tensor", "seq"),
        P("tensor", "seq"),
        P("tensor", "seq"),
        P("seq"),
        P("pipe", "seq", None),
        P("pipe", "tensor", None),
        P("pipe", None),
        P("pipe", None),
        P(),
    )
    return jax.shard_map(
        per_device, mesh=mesh, in_specs=placed, out_specs=P(("seq", "tensor")), check_vma=False
    )
```

time: 375 us -> 195 us (0.52)
  waiting for transfers between devices: 253 us -> 64.8 us
  starting transfers between devices: 0.12 us -> 57.6 us
  blocking collectives: 81 us -> 23.7 us
  local copies, waits for them, and re-layouts: 0.71 us -> 14.9 us
  between operations: 15.1 us -> 2.42 us
  other arithmetic: 3.46 us -> 7.36 us
    unnamed x5 -> x0, waiting for transfers between devices: 138 us -> none
    all_gather x1 -> x0, waiting for transfers between devices: 90 us -> none  [per_device(): gathered = lax.all_gather(hidden[0], 'seq', axis=0, tiled=True)]
    psum x3 -> x0, blocking collectives: 81 us -> none  [the longest x1 50.4 us: per_device(): summed = lax.psum(partial_value, 'pipe')]
    all_to_all x0 -> x6, waiting for transfers between devices: none -> 43.5 us  [the longest x2 20.6 us: per_device(): got = lax.all_to_all(sent, ('tensor', 'pipe'), 0, 0)]
    all_to_all x0 -> x6, starting transfers between devices: none -> 36.6 us  [the longest x2 16.6 us: per_device(): got = lax.all_to_all(sent, ('tensor', 'pipe'), 0, 0)]
    reduce_scatter x2 -> x0, waiting for transfers between devices: 24.7 us -> none  [the longest x1 24.6 us: per_device(): lax.psum_scatter(jnp.dot(gathered, weight, preferred_element_type=jnp.flo...]
    all_to_all x0 -> x2, blocking collectives: none -> 23.7 us  [the longest x1 14.7 us: per_device(): lax.all_to_all(partial_cores, ('seq', 'tensor'), 0, 0, tiled=True)]
    ppermute x0 -> x14, waiting for transfers between devices: none -> 21.3 us  [the longest x4 12.3 us: ring_blocks(): down_high = lax.ppermute(down_high, axis, down)]
  transfers between devices with their start and end apart: 4 -> 20, of which waited for: 3 -> 7; matrix products, arithmetic and copies ran while one was open for 2% -> 20% of each run, Pallas kernels for 0% -> 0%
where the time goes in v1:
time: 195 us; the launch traced here: 194 us
  waiting for transfers between devices  64.8 us (33%)
  starting transfers between devices  57.6 us (30%)
  blocking collectives  23.7 us (12%)
  matrix products  23.6 us (12%)
  local copies, waits for them, and re-layouts  14.9 us (8%)
  other arithmetic  7.36 us (4%)
  between operations  2.42 us (1%)
    all_to_all x2, waiting for transfers between devices, per_device(): got = lax.all_to_all(sent, ('tensor', 'pipe'), 0, 0)  20.6 us
    dot_general x5, matrix products, per_device(): jnp.dot(rows, weight, preferred_element_type=f32).astype(jnp.bfloat16)  20.3 us
    all_to_all x2, starting transfers between devices, per_device(): got = lax.all_to_all(sent, ('tensor', 'pipe'), 0, 0)  16.6 us
    all_to_all x1, blocking collectives, per_device(): lax.all_to_all(partial_cores, ('seq', 'tensor'), 0, 0, tiled=True)  14.7 us
    all_to_all x1, waiting for transfers between devices, per_device(): lax.all_to_all(jnp.broadcast_to(own_left[None], (layers, rank, width)), '...  14.4 us
    ppermute x4, waiting for transfers between devices, ring_blocks(): down_high = lax.ppermute(down_high, axis, down)  12.3 us
    ppermute x3, starting transfers between devices, ring_blocks(): down_low = lax.ppermute(down_low, axis, down)  9.29 us
    ppermute x4, starting transfers between devices, ring_blocks(): down_high = lax.ppermute(down_high, axis, down)  9.18 us
  transfers between devices with their start and end apart: 20, of which 7 were waited for; matrix products, arithmetic and copies ran while one was open for 20% of the time, Pallas kernels for 0%

profile of v1, /device:TPU:1, one launch (start us, length us, event | category | flops | bytes accessed | tf_op | source)
XLA Modules:
  0.0 194.4 jit_solution(12268309566204798117)
XLA Ops:
  4.6 3.9 %collective-permute-start.2 = (bf16[64,3584]{1,0:T(8,128)(2,1)}, bf16[64,3584]{1,0:T(8,128)(2,1)}, u32[]{:S(2)}, u32[]{:S(2)}) collective-permute-start(bf16[64,3584]{1,0:T(8,128)(2,1)} %get-tuple-element.11), channel_id=1, source_target_pairs={{0,28},{4,0},{8,4},{12,8},{16,12},{20,16},{24,20},{28,24},{1,29},{... | collective-permute-start | bytes 1376264 | tf_op jit(solution)/shard_map/ppermute | solution.py:21
  13.4 4.2 %all-to-all-start = ((bf16[4,2,2,4,1024]{4,3,2,1,0:T(4,128)(2,1)}), bf16[4,2,2,4,1024]{4,3,2,1,0:T(4,128)(2,1)S(1)}, u32[]{:S(2)}, u32[]{:S(2)}) async-start(bf16[4,2,2,4,1024]{4,3,2,1,0:T(4,128)(2,1)} %copy_bitcast_fusion), calls=%async_computation | async-start | bytes 262144 | tf_op jit(solution)/shard_map/all_to_all | solution.py:65
  17.6 4.2 %fusion.46 = bf16[128,1024]{1,0:T(8,128)(2,1)S(1)} fusion(bf16[1,3584,1024]{2,1,0:T(8,128)(2,1)} %param.11, bf16[1,128,3584]{2,1,0:T(8,128)(2,1)S(1)} %copy-done.1), kind=kOutput, calls=%fused_computation.37 | convolution fusion | flops 939655168 | bytes 8519680 | tf_op jit(solution)/shard_map/dot_general | solution.py:74
  25.1 3.9 %collective-permute-done.1 = bf16[64,3584]{1,0:T(8,128)(2,1)} collective-permute-done((bf16[64,3584]{1,0:T(8,128)(2,1)S(1)}, bf16[64,3584]{1,0:T(8,128)(2,1)}, u32[]{:S(2)}, u32[]{:S(2)}) %collective-permute-start.1) | collective-permute-done | bytes 458784 | tf_op jit(solution)/shard_map/ppermute | solution.py:20
  28.9 2.7 %collective-permute-start.6 = (bf16[64,3584]{1,0:T(8,128)(2,1)}, bf16[64,3584]{1,0:T(8,128)(2,1)}, u32[]{:S(2)}, u32[]{:S(2)}) collective-permute-start(bf16[64,3584]{1,0:T(8,128)(2,1)} %collective-permute-done.2), channel_id=1, source_target_pairs={{0,28},{4,0},{8,4},{12,8},{16,12},{20,16},{24,20},{28,24},{1,29},{... | collective-permute-start | bytes 1376264 | tf_op jit(solution)/shard_map/ppermute | solution.py:21
  31.7 5.7 %fusion.31 = bf16[256,1024]{1,0:T(8,128)(2,1)S(1)} fusion(bf16[1,3584,1024]{2,1,0:T(8,128)(2,1)} %param.11, bf16[64,3584]{1,0:T(8,128)(2,1)} %collective-permute-done.3, bf16[64,3584]{1,0:T(8,128)(2,1)} %collective-permute-done.2, bf16[64,3584]{1,0:T(8,128)(2,1)} %collective-permute-done.1, bf16[64,3584]{1,0:T(8,128)(2,1)} %collective-permute-done), kind=kOutput, calls=%fused_computation.34 | convolution fusion | flops 1886650368 | bytes 9699328 | tf_op jit(solution)/shard_map/dot_general | solution.py:74
  37.4 12.3 %collective-permute-done.7 = bf16[64,3584]{1,0:T(8,128)(2,1)} collective-permute-done((bf16[64,3584]{1,0:T(8,128)(2,1)}, bf16[64,3584]{1,0:T(8,128)(2,1)}, u32[]{:S(2)}, u32[]{:S(2)}) %collective-permute-start.7) | collective-permute-done | bytes 458784 | tf_op jit(solution)/shard_map/ppermute | solution.py:19
  49.7 3.4 %collective-permute-start.11 = (bf16[64,3584]{1,0:T(8,128)(2,1)}, bf16[64,3584]{1,0:T(8,128)(2,1)}, u32[]{:S(2)}, u32[]{:S(2)}) collective-permute-start(bf16[64,3584]{1,0:T(8,128)(2,1)} %collective-permute-done.7), channel_id=1, source_target_pairs={{0,28},{4,0},{8,4},{12,8},{16,12},{20,16},{24,20},{28,24},{1,29},{... | collective-permute-start | bytes 1376264 | tf_op jit(solution)/shard_map/ppermute | solution.py:19
  55.8 3.5 %fusion.36 = bf16[256,1024]{1,0:T(8,128)(2,1)S(1)} fusion(bf16[1,3584,1024]{2,1,0:T(8,128)(2,1)S(1)} %bitcast.128, bf16[64,3584]{1,0:T(8,128)(2,1)} %collective-permute-done.7, bf16[64,3584]{1,0:T(8,128)(2,1)} %collective-permute-done.6, bf16[64,3584]{1,0:T(8,128)(2,1)} %collective-permute-done.5, bf16[64,3584]{1,0:T(8,128)(2,1)} %collective-permute-done.4), kind=kOutput, calls=%fused_computation.35 | convolution fusion | flops 1886650368 | bytes 9699328 | tf_op jit(solution)/shard_map/dot_general | solution.py:74
  62.2 11.0 %all-to-all-start.1 = ((bf16[32,20,1024]{2,1,0:T(8,128)(2,1)}), bf16[32,20,1024]{2,1,0:T(8,128)(2,1)}, u32[]{:S(2)}, u32[]{:S(2)}) async-start(bf16[32,20,1024]{2,1,0:T(8,128)(2,1)} %copy.66), calls=%async_computation.1 | async-start | bytes 3145728 | tf_op jit(solution)/shard_map/all_to_all | solution.py:82
  73.4 3.0 %collective-permute-start.13 = (bf16[64,3584]{1,0:T(8,128)(2,1)}, bf16[64,3584]{1,0:T(8,128)(2,1)S(1)}, u32[]{:S(2)}, u32[]{:S(2)}) collective-permute-start(bf16[64,3584]{1,0:T(8,128)(2,1)} %collective-permute-done.11), channel_id=1, source_target_pairs={{0,28},{4,0},{8,4},{12,8},{16,12},{20,16},{24,20},{28,24},{1,29},{... | collective-permute-start | bytes 1376264 | tf_op jit(solution)/shard_map/ppermute | solution.py:24
  76.4 5.7 %fusion.41 = bf16[256,1024]{1,0:T(8,128)(2,1)S(1)} fusion(bf16[1,3584,1024]{2,1,0:T(8,128)(2,1)} %param.11, bf16[64,3584]{1,0:T(8,128)(2,1)} %collective-permute-done.11, bf16[64,3584]{1,0:T(8,128)(2,1)} %collective-permute-done.10, bf16[64,3584]{1,0:T(8,128)(2,1)} %collective-permute-done.9, bf16[64,3584]{1,0:T(8,128)(2,1)} %collective-permute-done.8), kind=kOutput, calls=%fused_computation.36 | convolution fusion | flops 1886650368 | bytes 9699328 | tf_op jit(solution)/shard_map/dot_general | solution.py:74
  82.2 5.1 %collective-permute-done.12 = bf16[64,3584]{1,0:T(8,128)(2,1)S(1)} collective-permute-done((bf16[64,3584]{1,0:T(8,128)(2,1)}, bf16[64,3584]{1,0:T(8,128)(2,1)S(1)}, u32[]{:S(2)}, u32[]{:S(2)}) %collective-permute-start.12) | collective-permute-done | bytes 458784 | tf_op jit(solution)/shard_map/ppermute | solution.py:23
  90.5 5.0 %all-to-all-done.1 = bf16[32,20,1024]{2,1,0:T(8,128)(2,1)} async-done(((bf16[32,20,1024]{2,1,0:T(8,128)(2,1)}), bf16[32,20,1024]{2,1,0:T(8,128)(2,1)}, u32[]{:S(2)}, u32[]{:S(2)}) %all-to-all-start.1) | async-done | bytes 1310752 | tf_op jit(solution)/shard_map/all_to_all | solution.py:82
  95.5 5.6 %all-to-all-start.2 = ((bf16[32,12,1024]{2,1,0:T(8,128)(2,1)}), bf16[32,12,1024]{2,1,0:T(8,128)(2,1)S(1)}, u32[]{:S(2)}, u32[]{:S(2)}) async-start(bf16[32,12,1024]{2,1,0:T(8,128)(2,1)} %copy.68), calls=%async_computation.2 | async-start | bytes 2097152 | tf_op jit(solution)/shard_map/all_to_all | solution.py:82
  102.9 15.5 %all-to-all-done.2 = bf16[32,12,1024]{2,1,0:T(8,128)(2,1)S(1)} async-done(((bf16[32,12,1024]{2,1,0:T(8,128)(2,1)}), bf16[32,12,1024]{2,1,0:T(8,128)(2,1)S(1)}, u32[]{:S(2)}, u32[]{:S(2)}) %all-to-all-start.2) | async-done | bytes 786464 | tf_op jit(solution)/shard_map/all_to_all | solution.py:82
  119.5 4.0 %all-to-all-start.3 = ((f32[8,32,1024]{2,1,0:T(8,128)}), f32[8,32,1024]{2,1,0:T(8,128)S(1)}, u32[]{:S(2)}, u32[]{:S(2)}) async-start(f32[8,32,1024]{2,1,0:T(8,128)} %broadcast_in_dim.18), calls=%async_computation.3 | async-start | bytes 2097152 | tf_op jit(solution)/shard_map/all_to_all | solution.py:58
  124.2 14.4 %all-to-all-done.3 = f32[8,32,1024]{2,1,0:T(8,128)S(1)} async-done(((f32[8,32,1024]{2,1,0:T(8,128)}), f32[8,32,1024]{2,1,0:T(8,128)S(1)}, u32[]{:S(2)}, u32[]{:S(2)}) %all-to-all-start.3) | async-done | bytes 1048608 | tf_op jit(solution)/shard_map/all_to_all | solution.py:58
  138.6 3.5 %all-to-all-start.5 = ((f32[4,1,1024]{2,1,0:T(1,128)}), f32[4,1,1024]{2,1,0:T(1,128)S(1)}, u32[]{:S(2)}, u32[]{:S(2)}) async-start(f32[4,1,1024]{2,1,0:T(1,128)} %reshape.124), calls=%async_computation.5 | async-start | bytes 32768 | tf_op jit(solution)/shard_map/all_to_all | solution.py:54
  142.1 2.7 %convolution_bitcast_fusion = f32[8,8,4,2,32]{4,1,0,2,3:T(8,128)S(1)} fusion(f32[8,32,1024]{2,1,0:T(8,128)S(1)} %all-to-all-done.3, f32[2,8,4,1024,1]{3,2,1,0,4:T(4,128)S(1)} %bitcast.137), kind=kOutput, calls=%fused_computation.39 | convolution fusion | flops 201326592 | bytes 1376256 | tf_op jit(solution)/shard_map/dot_general | solution.py:93
  146.6 8.4 %all-to-all-start.4 = ((f32[64,4,66]{2,1,0:T(4,128)}), f32[64,4,66]{2,1,0:T(4,128)S(1)}, u32[]{:S(2)}, u32[]{:S(2)}) async-start(f32[64,4,66]{2,1,0:T(4,128)} %copy.74), calls=%async_computation.4 | async-start | bytes 262144 | tf_op jit(solution)/shard_map/all_to_all | solution.py:107
  156.5 8.5 %all-to-all-done.4 = f32[64,4,66]{2,1,0:T(4,128)S(1)} async-done(((f32[64,4,66]{2,1,0:T(4,128)}), f32[64,4,66]{2,1,0:T(4,128)S(1)}, u32[]{:S(2)}, u32[]{:S(2)}) %all-to-all-start.4) | async-done | bytes 67616 | tf_op jit(solution)/shard_map/all_to_all | solution.py:107
  166.1 14.7 %all_to_all.45 = f32[32,1,1024]{2,1,0:T(1,128)S(1)} all-to-all(f32[32,1,1024]{2,1,0:T(1,128)S(1)} %copy.77), channel_id=1, replica_groups=mesh['pipe'=8,'seq'=8,'tensor'=4] {'seq','tensor'}, dimensions={0} | all-to-all | bytes 262144 | tf_op jit(solution)/shard_map/all_to_all | solution.py:125
  182.9 9.1 %all_to_all.46 = f32[8,1,2]{2,1,0:T(1,128)S(1)} all-to-all(f32[8,1,2]{2,1,0:T(1,128)S(1)} %broadcast_in_dim.25), channel_id=1, replica_groups=mesh['pipe'=8,'seq'=8,'tensor'=4] {'pipe'}, dimensions={0} | all-to-all | bytes 128 | tf_op jit(solution)/shard_map/all_to_all | solution.py:129
  (132 shorter events, 32.0 us)
Async XLA Ops:
  2.1 22.9 %collective-permute-start = (bf16[64,3584]{1,0:T(8,128)(2,1)}, bf16[64,3584]{1,0:T(8,128)(2,1)}, u32[]{:S(2)}, u32[]{:S(2)}) collective-permute-start(bf16[64,3584]{1,0:T(8,128)(2,1)} %get-tuple-element.11), channel_id=1, source_target_pairs={{0,4},{4,8},{8,12},{12,16},{16,20},{20,24},{24,28},{28,0},{1,5},{5... | collective-permute-start | bytes 1376264 | tf_op jit(solution)/shard_map/ppermute | solution.py:18
  4.6 24.3 %collective-permute-start.2 = (bf16[64,3584]{1,0:T(8,128)(2,1)}, bf16[64,3584]{1,0:T(8,128)(2,1)}, u32[]{:S(2)}, u32[]{:S(2)}) collective-permute-start(bf16[64,3584]{1,0:T(8,128)(2,1)} %get-tuple-element.11), channel_id=1, source_target_pairs={{0,28},{4,0},{8,4},{12,8},{16,12},{20,16},{24,20},{28,24},{1,29},{... | collective-permute-start | bytes 1376264 | tf_op jit(solution)/shard_map/ppermute | solution.py:21
  8.5 20.4 %collective-permute-start.1 = (bf16[64,3584]{1,0:T(8,128)(2,1)S(1)}, bf16[64,3584]{1,0:T(8,128)(2,1)}, u32[]{:S(2)}, u32[]{:S(2)}) collective-permute-start(bf16[64,3584]{1,0:T(8,128)(2,1)S(1)} %get-tuple-element.12), channel_id=1, source_target_pairs={{0,4},{4,8},{8,12},{12,16},{16,20},{20,24},{24,28},{28,0},{1,5},{5... | collective-permute-start | bytes 1376264 | tf_op jit(solution)/shard_map/ppermute | solution.py:20
  8.5 23.1 %collective-permute-start.3 = (bf16[64,3584]{1,0:T(8,128)(2,1)S(1)}, bf16[64,3584]{1,0:T(8,128)(2,1)}, u32[]{:S(2)}, u32[]{:S(2)}) collective-permute-start(bf16[64,3584]{1,0:T(8,128)(2,1)S(1)} %get-tuple-element.12), channel_id=1, source_target_pairs={{0,28},{4,0},{8,4},{12,8},{16,12},{20,16},{24,20},{28,24},{1,29},{... | collective-permute-start | bytes 1376264 | tf_op jit(solution)/shard_map/ppermute | solution.py:19
  13.4 9.5 %all-to-all-start = ((bf16[4,2,2,4,1024]{4,3,2,1,0:T(4,128)(2,1)}), bf16[4,2,2,4,1024]{4,3,2,1,0:T(4,128)(2,1)S(1)}, u32[]{:S(2)}, u32[]{:S(2)}) async-start(bf16[4,2,2,4,1024]{4,3,2,1,0:T(4,128)(2,1)} %copy_bitcast_fusion), calls=%async_computation | async-start | bytes 262144 | tf_op jit(solution)/shard_map/all_to_all | solution.py:65
  24.4 31.4 %slice-start = ((s8[7340032]{0:T(1024)(128)(4,1)}), s8[4194304]{0:T(1024)(128)(4,1)S(1)}, s32[]{:S(2)}) async-start(s8[7340032]{0:T(1024)(128)(4,1)} %bitcast.127), calls=%async_computation.8 | async-start | bytes 8388608
  25.1 28.0 %collective-permute-start.4 = (bf16[64,3584]{1,0:T(8,128)(2,1)}, bf16[64,3584]{1,0:T(8,128)(2,1)}, u32[]{:S(2)}, u32[]{:S(2)}) collective-permute-start(bf16[64,3584]{1,0:T(8,128)(2,1)} %collective-permute-done), channel_id=1, source_target_pairs={{0,4},{4,8},{8,12},{12,16},{16,20},{20,24},{24,28},{28,0},{1,5},{5... | collective-permute-start | bytes 1376264 | tf_op jit(solution)/shard_map/ppermute | solution.py:18
  28.9 26.8 %collective-permute-start.5 = (bf16[64,3584]{1,0:T(8,128)(2,1)}, bf16[64,3584]{1,0:T(8,128)(2,1)}, u32[]{:S(2)}, u32[]{:S(2)}) collective-permute-start(bf16[64,3584]{1,0:T(8,128)(2,1)} %collective-permute-done.1), channel_id=1, source_target_pairs={{0,4},{4,8},{8,12},{12,16},{16,20},{20,24},{24,28},{28,0},{1,5},{5... | collective-permute-start | bytes 1376264 | tf_op jit(solution)/shard_map/ppermute | solution.py:20
  28.9 24.2 %collective-permute-start.6 = (bf16[64,3584]{1,0:T(8,128)(2,1)}, bf16[64,3584]{1,0:T(8,128)(2,1)}, u32[]{:S(2)}, u32[]{:S(2)}) collective-permute-start(bf16[64,3584]{1,0:T(8,128)(2,1)} %collective-permute-done.2), channel_id=1, source_target_pairs={{0,28},{4,0},{8,4},{12,8},{16,12},{20,16},{24,20},{28,24},{1,29},{... | collective-permute-start | bytes 1376264 | tf_op jit(solution)/shard_map/ppermute | solution.py:21
  31.6 18.1 %collective-permute-start.7 = (bf16[64,3584]{1,0:T(8,128)(2,1)}, bf16[64,3584]{1,0:T(8,128)(2,1)}, u32[]{:S(2)}, u32[]{:S(2)}) collective-permute-start(bf16[64,3584]{1,0:T(8,128)(2,1)} %collective-permute-done.3), channel_id=1, source_target_pairs={{0,28},{4,0},{8,4},{12,8},{16,12},{20,16},{24,20},{28,24},{1,29},{... | collective-permute-start | bytes 1376264 | tf_op jit(solution)/shard_map/ppermute | solution.py:19
  49.7 23.7 %collective-permute-start.11 = (bf16[64,3584]{1,0:T(8,128)(2,1)}, bf16[64,3584]{1,0:T(8,128)(2,1)}, u32[]{:S(2)}, u32[]{:S(2)}) collective-permute-start(bf16[64,3584]{1,0:T(8,128)(2,1)} %collective-permute-done.7), channel_id=1, source_target_pairs={{0,28},{4,0},{8,4},{12,8},{16,12},{20,16},{24,20},{28,24},{1,29},{... | collective-permute-start | bytes 1376264 | tf_op jit(solution)/shard_map/ppermute | solution.py:19
  53.1 20.2 %collective-permute-start.8 = (bf16[64,3584]{1,0:T(8,128)(2,1)}, bf16[64,3584]{1,0:T(8,128)(2,1)}, u32[]{:S(2)}, u32[]{:S(2)}) collective-permute-start(bf16[64,3584]{1,0:T(8,128)(2,1)} %collective-permute-done.4), channel_id=1, source_target_pairs={{0,4},{4,8},{8,12},{12,16},{16,20},{20,24},{24,28},{28,0},{1,5},{5... | collective-permute-start | bytes 1376264 | tf_op jit(solution)/shard_map/ppermute | solution.py:18
  53.1 23.3 %collective-permute-start.10 = (bf16[64,3584]{1,0:T(8,128)(2,1)}, bf16[64,3584]{1,0:T(8,128)(2,1)}, u32[]{:S(2)}, u32[]{:S(2)}) collective-permute-start(bf16[64,3584]{1,0:T(8,128)(2,1)} %collective-permute-done.6), channel_id=1, source_target_pairs={{0,28},{4,0},{8,4},{12,8},{16,12},{20,16},{24,20},{28,24},{1,29},{... | collective-permute-start | bytes 1376264 | tf_op jit(solution)/shard_map/ppermute | solution.py:21
  55.8 20.7 %collective-permute-start.9 = (bf16[64,3584]{1,0:T(8,128)(2,1)}, bf16[64,3584]{1,0:T(8,128)(2,1)}, u32[]{:S(2)}, u32[]{:S(2)}) collective-permute-start(bf16[64,3584]{1,0:T(8,128)(2,1)} %collective-permute-done.5), channel_id=1, source_target_pairs={{0,4},{4,8},{8,12},{12,16},{16,20},{20,24},{24,28},{28,0},{1,5},{5... | collective-permute-start | bytes 1376264 | tf_op jit(solution)/shard_map/ppermute | solution.py:20
  62.2 33.3 %all-to-all-start.1 = ((bf16[32,20,1024]{2,1,0:T(8,128)(2,1)}), bf16[32,20,1024]{2,1,0:T(8,128)(2,1)}, u32[]{:S(2)}, u32[]{:S(2)}) async-start(bf16[32,20,1024]{2,1,0:T(8,128)(2,1)} %copy.66), calls=%async_computation.1 | async-start | bytes 3145728 | tf_op jit(solution)/shard_map/all_to_all | solution.py:82
  73.3 14.0 %collective-permute-start.12 = (bf16[64,3584]{1,0:T(8,128)(2,1)}, bf16[64,3584]{1,0:T(8,128)(2,1)S(1)}, u32[]{:S(2)}, u32[]{:S(2)}) collective-permute-start(bf16[64,3584]{1,0:T(8,128)(2,1)} %collective-permute-done.8), channel_id=1, source_target_pairs={{0,4},{4,8},{8,12},{12,16},{16,20},{20,24},{24,28},{28,0},{1,5},{5... | collective-permute-start | bytes 1376264 | tf_op jit(solution)/shard_map/ppermute | solution.py:23
  73.4 13.9 %collective-permute-start.13 = (bf16[64,3584]{1,0:T(8,128)(2,1)}, bf16[64,3584]{1,0:T(8,128)(2,1)S(1)}, u32[]{:S(2)}, u32[]{:S(2)}) collective-permute-start(bf16[64,3584]{1,0:T(8,128)(2,1)} %collective-permute-done.11), channel_id=1, source_target_pairs={{0,28},{4,0},{8,4},{12,8},{16,12},{20,16},{24,20},{28,24},{1,29},{... | collective-permute-start | bytes 1376264 | tf_op jit(solution)/shard_map/ppermute | solution.py:24
  95.5 22.9 %all-to-all-start.2 = ((bf16[32,12,1024]{2,1,0:T(8,128)(2,1)}), bf16[32,12,1024]{2,1,0:T(8,128)(2,1)S(1)}, u32[]{:S(2)}, u32[]{:S(2)}) async-start(bf16[32,12,1024]{2,1,0:T(8,128)(2,1)} %copy.68), calls=%async_computation.2 | async-start | bytes 2097152 | tf_op jit(solution)/shard_map/all_to_all | solution.py:82
  119.5 19.1 %all-to-all-start.3 = ((f32[8,32,1024]{2,1,0:T(8,128)}), f32[8,32,1024]{2,1,0:T(8,128)S(1)}, u32[]{:S(2)}, u32[]{:S(2)}) async-start(f32[8,32,1024]{2,1,0:T(8,128)} %broadcast_in_dim.18), calls=%async_computation.3 | async-start | bytes 2097152 | tf_op jit(solution)/shard_map/all_to_all | solution.py:58
  124.1 30.9 %copy-start.11 = (s32[32]{0:T(128)S(1)}, s32[32]{0:T(128)}, u32[]{:S(2)}) copy-start(s32[32]{0:T(128)} %param.19) | copy-start | bytes 388
  138.6 8.0 %all-to-all-start.5 = ((f32[4,1,1024]{2,1,0:T(1,128)}), f32[4,1,1024]{2,1,0:T(1,128)S(1)}, u32[]{:S(2)}, u32[]{:S(2)}) async-start(f32[4,1,1024]{2,1,0:T(1,128)} %reshape.124), calls=%async_computation.5 | async-start | bytes 32768 | tf_op jit(solution)/shard_map/all_to_all | solution.py:54
  144.8 36.1 %copy-start.9 = (f32[1,1024]{1,0:T(1,128)S(1)}, f32[1,1024]{1,0:T(1,128)}, u32[]{:S(2)}) copy-start(f32[1,1024]{1,0:T(1,128)} %param.17) | copy-start | bytes 12292
  144.8 36.1 %copy-start.10 = (f32[1,1024]{1,0:T(1,128)S(1)}, f32[1,1024]{1,0:T(1,128)}, u32[]{:S(2)}) copy-start(f32[1,1024]{1,0:T(1,128)} %param.18) | copy-start | bytes 12292
  146.6 18.3 %all-to-all-start.4 = ((f32[64,4,66]{2,1,0:T(4,128)}), f32[64,4,66]{2,1,0:T(4,128)S(1)}, u32[]{:S(2)}, u32[]{:S(2)}) async-start(f32[64,4,66]{2,1,0:T(4,128)} %copy.74), calls=%async_computation.4 | async-start | bytes 262144 | tf_op jit(solution)/shard_map/all_to_all | solution.py:107
  (12 other events, 190.3 us)

commit v2 on v0

v2 whole, which is shorter than its diff:
```python
import functools

import jax
import jax.numpy as jnp
from jax import lax
from jax.experimental import pallas as pl
from jax.experimental.pallas import tpu as pltpu
from jax.sharding import PartitionSpec as P

D = 8192
F32 = jnp.float32
BF16 = jnp.bfloat16
VMEM_BYTES = 16 << 20
PRODUCT_BYTES = 28 << 20
TILES = 4


def exact_dot(a, b, dims):
    return lax.dot_general(
        a, b, (dims, ((), ())), precision=lax.Precision.HIGHEST, preferred_element_type=F32
    )


def product_kernel(count, extras, based, *refs):
    pieces, weight, order, refs = refs[:count], refs[count], refs[count + 1], refs[count + 2 :]
    extra, refs = refs[: 2 * extras], refs[2 * extras :]
    base, refs = (refs[0], refs[1:]) if based else (None, refs)
    out, rows, tiles, total, sems, tile_sems = refs
    depth = tiles.shape[1]

    def fetch(k):
        return pltpu.make_async_copy(
            weight.at[pl.ds(k * depth, depth)], tiles.at[k], tile_sems.at[k]
        )

    copies, first = [], 0
    for k, piece in enumerate(pieces):
        size = piece.shape[0]
        copies.append(pltpu.make_async_copy(piece, rows.at[pl.ds(first, size)], sems.at[k]))
        first += size
    fetch(0).start()
    for copy in copies:
        copy.start()
    for k in range(1, TILES):
        fetch(k).start()
    for copy in copies:
        copy.wait()
    for k in range(TILES):
        fetch(k).wait()
        value = jnp.dot(
            rows[:, k * depth : (k + 1) * depth], tiles[k], preferred_element_type=F32
        )
        if k == 0:
            total[...] = value
        elif k < TILES - 1:
            total[...] += value
    value = (total[...] + value).astype(BF16)
    value = jnp.dot(order[...], value, preferred_element_type=F32)
    for k in range(extras):
        value += jnp.dot(extra[2 * k][...], extra[2 * k + 1][...], preferred_element_type=F32)
    if based:
        value += base[...].astype(F32)
    out[...] = value.astype(BF16)


def product(pieces, weight, order, extra=(), base=None):
    total = sum(p.shape[0] for p in pieces)
    depth, width = weight.shape
    height = order.shape[0]
    anywhere, held = pl.BlockSpec(memory_space=pl.ANY), pl.BlockSpec(memory_space=pltpu.VMEM)
    weight = pltpu.with_memory_space_constraint(weight, pltpu.HBM)
    small = [order, *extra] + ([] if base is None else [base])
    return pl.pallas_call(
        functools.partial(product_kernel, len(pieces), len(extra) // 2, base is not None),
        out_shape=jax.ShapeDtypeStruct((height, width), BF16),
        in_specs=[anywhere] * len(pieces) + [pl.BlockSpec(memory_space=pltpu.HBM)] + [held] * len(small),
        out_specs=held,
        scratch_shapes=[
            pltpu.VMEM((total, depth), BF16),
            pltpu.VMEM((TILES, depth // TILES, width), BF16),
            pltpu.VMEM((total, width), F32),
            pltpu.SemaphoreType.DMA((len(pieces),)),
            pltpu.SemaphoreType.DMA((TILES,)),
        ],
        compiler_params=pltpu.CompilerParams(vmem_limit_bytes=PRODUCT_BYTES),
        cost_estimate=pl.CostEstimate(flops=1 << 20, bytes_accessed=1 << 16, transcendentals=0),
    )(*pieces, weight, *small)


def reduce_rows(got, resid, aim, left, height):
    stream = resid[...] + jnp.sum(got[...].astype(F32), axis=0)
    square = jnp.sum(stream * stream, axis=1, keepdims=True)
    inner = jnp.sum(aim[...] * stream, axis=1, keepdims=True)
    lane = lax.broadcasted_iota(jnp.int32, (height, 128), 1)
    moments = jnp.where(lane == 0, square, jnp.where(lane == 1, inner, 0.0))
    return exact_dot(stream, left[...], ((1,), (1,))), moments


def stats_kernel(got, resid, aim, left, projected, moments):
    projected[...], moments[...] = reduce_rows(got, resid, aim, left, moments.shape[0])


def stats(got, resid, aim, left):
    count = got.shape[1]
    return pl.pallas_call(
        stats_kernel,
        out_shape=(
            jax.ShapeDtypeStruct((count, left.shape[0]), F32),
            jax.ShapeDtypeStruct((count, 128), F32),
        ),
        compiler_params=pltpu.CompilerParams(vmem_limit_bytes=VMEM_BYTES),
    )(got, resid, aim, left)


def pack_kernel(
    layers, share, got, resid, aim, left, first, first_moments, target, order, packed
):
    projected, moments = reduce_rows(got, resid, aim, left, got.shape[1])
    projected = jnp.concatenate([first[...], projected], axis=0)
    moments = jnp.concatenate([first_moments[...], moments], axis=0)
    projected = exact_dot(order[...], projected, ((1,), (0,)))
    moments = exact_dot(order[...], moments, ((1,), (0,)))
    blocks = order.shape[0] // share
    rank = left.shape[0] // layers
    lane = lax.broadcasted_iota(jnp.int32, (blocks, 128), 1)
    sums = jnp.zeros((blocks, 128), F32)
    for i in range(share):
        part = moments[i * blocks : (i + 1) * blocks]
        sums = jnp.where(lane == i, part[:, 0:1], sums)
        sums = jnp.where(lane == share + i, part[:, 1:2], sums)
    for l in range(layers):
        place = pl.ds(l * blocks, blocks)
        for k, source in enumerate((projected, target[...])):
            packed[place, 0, k * 128 : (k + 1) * 128] = jnp.concatenate(
                [
                    source[i * blocks : (i + 1) * blocks, l * rank : (l + 1) * rank]
                    for i in range(share)
                ],
                axis=1,
            )
        packed[place, 0, 256:384] = sums


def pack(layers, share, *operands):
    blocks = operands[-1].shape[0] // share
    return pl.pallas_call(
        functools.partial(pack_kernel, layers, share),
        out_shape=jax.ShapeDtypeStruct((layers * blocks, 1, 384), F32),
        compiler_params=pltpu.CompilerParams(vmem_limit_bytes=VMEM_BYTES),
    )(*operands)


def per_device(
    hidden, down_weight, resid, target, gain, query_left, query_right, query_core, eigen, lengths
):
    layers = lax.axis_size("pipe")
    seqs = lax.axis_size("seq")
    tensors = lax.axis_size("tensor")
    layer = lax.axis_index("pipe")
    seq = lax.axis_index("seq")
    tensor = lax.axis_index("tensor")
    own = hidden[0]
    width = down_weight.shape[2]
    block_rows = own.shape[0]
    rank = query_left.shape[2]
    peers = tensors * layers
    share = block_rows // peers
    strip = share * layers
    local_blocks = seqs // tensors
    half = block_rows // 2
    up = [(i, (i + 1) % seqs) for i in range(seqs)]
    down = [(i, (i - 1) % seqs) for i in range(seqs)]
    tie = lax.optimization_barrier

    def move(pair):
        return lax.ppermute(pair[0], "seq", up), lax.ppermute(pair[1], "seq", down)

    def column(n):
        return jnp.arange(n, dtype=jnp.int32)

    def one_hot(source, count):
        return (source[:, None] == column(count)[None, :]).astype(BF16)

    def layout(slots):
        place = column(peers * slots * share)
        return place // (slots * share), place // share % slots, place % share

    def units(slots, first, count):
        peer, slot, line = layout(slots)
        source = (slot - first) * block_rows + peer * share + line
        inside = (slot >= first) & (slot < first + count)
        return one_hot(jnp.where(inside, source, -1), count * block_rows)

    def exchange(sent):
        return lax.all_to_all(sent.reshape(peers, -1, width), ("tensor", "pipe"), 0, 0)

    low, high = own[:half], own[half:]
    a1 = move((low, high))
    left_own = jnp.broadcast_to(
        jnp.transpose(query_left[0])[None], (layers, rank, width)
    )
    low, high, left_own = tie((low, high, left_own))
    b1 = move((high, low))
    left_all = lax.all_to_all(left_own, "pipe", 0, 0).reshape(layers * rank, width)
    weight = down_weight[0]
    aside = jnp.where(layer // (2 * local_blocks) == 0, resid, target)
    aside = lax.dynamic_slice_in_dim(aside, layer // 2 % local_blocks * block_rows, block_rows, 0)
    right_partial = jnp.dot(own, query_right[0], preferred_element_type=F32)
    right_partial = right_partial.reshape(tensors, strip * rank)
    right_high = lax.reduce_precision(right_partial, 8, 7)
    right_low = (right_partial - right_high).astype(BF16)
    right_rows = jnp.concatenate([right_high.astype(BF16), right_low], axis=0)
    right_rows = jnp.pad(right_rows, ((0, 128 - 2 * tensors), (0, 0)))

    near = 3
    peer, slot, line = layout(near + 1)
    spare = (slot == near) & (line < 2)
    aside_order = one_hot(
        jnp.where(spare, peer * share + layer % 2 * 2 + line, -1), block_rows
    )
    right_order = one_hot(
        jnp.where(spare & (peer % layers == layer), line * tensors + peer // layers, -1), 128
    )
    near_order, middle_order = units(near + 1, 0, 3), units(2, 0, 2)
    pair_order, last_order = units(near + 1, 0, 2), units(near + 1, 2, 1)
    near_order, middle_order, pair_order, last_order, aside_order, right_order, a1, aside = tie(
        (near_order, middle_order, pair_order, last_order, aside_order, right_order, a1, aside)
    )

    a2 = move(a1)
    b1, right_rows = tie((b1, right_rows))
    b2 = move(b1)
    sent = product(
        [own, a1[0], a1[1], b1[1], b1[0]], weight, near_order, (aside_order, aside)
    )
    a2, sent, left_all = tie((a2, sent, left_all))
    got_near = exchange(sent)
    a3 = move(a2)
    b3 = move(b2)
    sent = product([a2[0], a2[1], b2[1], b2[0]], weight, middle_order)
    a3, sent = tie((a3, sent))
    a4 = move(a3)
    b3, sent, got_near = tie((b3, sent, got_near))
    got_middle = exchange(sent)
    sent = product(
        [a3[0], a3[1], b3[1], b3[0]], weight, pair_order, (right_order, right_rows)
    )
    a4, sent, got_middle = tie((a4, sent, got_middle))
    got_far = exchange(product(list(a4), weight, last_order, base=sent))

    turned = jnp.where(tensor < tensors // 2, 1, -1)
    slots = [0, -1, 1, None, -2, 2, -3, 3, seqs // 2, None]
    slot = column(len(slots) * share)
    offset = jnp.zeros_like(slot)
    filled = jnp.ones_like(slot)
    for i, o in enumerate(slots):
        if o is None:
            filled = jnp.where(slot // share == i, 0, filled)
        else:
            offset = jnp.where(slot // share == i, o * turned, offset)
    block = (seq + offset + 2 * seqs) % seqs
    in_order = jnp.where(filled == 1, block * share + slot % share, -1)
    turn = in_order[:, None] == column(seqs * share)[None, :]
    by_line = jnp.where(filled == 1, slot % share * seqs + block, -1)
    order = (column(seqs * share)[:, None] == by_line[None, :]).astype(F32)

    both = got_near[:, near * share : near * share + 2].reshape(
        tensors, 2, local_blocks * share, width
    )
    both = jnp.transpose(both, (1, 0, 2, 3)).reshape(2, seqs * share, width)
    turn = turn.astype(BF16)
    resid_rows = jnp.dot(turn, both[0], preferred_element_type=F32)
    aim_rows = gain[None, :] * jnp.dot(turn, both[1], preferred_element_type=F32)
    right_proj = jnp.sum(got_far[:, near * share : near * share + 2].astype(F32), axis=(0, 1))
    right_proj = right_proj.reshape(strip, rank)
    got_first = jnp.concatenate([got_near, got_middle], axis=1)
    cut = got_first.shape[1]
    first = stats(got_first, resid_rows[:cut], aim_rows[:cut], left_all)
    target_proj = exact_dot(order, exact_dot(aim_rows, left_all, ((1,), (1,))), ((1,), (0,)))
    packed = pack(
        layers,
        share,
        got_far,
        resid_rows[cut:],
        aim_rows[cut:],
        left_all,
        first[0],
        first[1],
        target_proj,
        order,
    )
    packed = lax.all_to_all(packed, ("pipe", "seq"), 0, 0)
    totals = jnp.sum(packed.reshape(layers, seqs, packed.shape[2]), axis=1)
    cut = share * rank
    stream_proj = totals[:, :cut].reshape(strip, rank)
    target_proj = totals[:, cut : 2 * cut].reshape(strip, rank)
    square_sum = totals[:, 2 * cut : 2 * cut + share].reshape(strip, 1)
    inner = totals[:, 2 * cut + share : 2 * cut + 2 * share].reshape(strip, 1)
    root = jnp.sqrt(square_sum / D + 1e-05)
    left_proj = target_proj / root - stream_proj * (inner / (D * root * root * root))

    outer = (left_proj[:, :, None] * right_proj[:, None, :]).reshape(strip, rank * rank)
    number = jnp.arange(lengths.shape[0], dtype=jnp.int32)
    starts = jnp.sum(jnp.where(number[None, :] < number[:, None], lengths[None, :], 0), axis=1)
    ends = starts + lengths
    token = seq * block_rows + tensor * strip + jnp.arange(strip, dtype=jnp.int32)
    member = ((token[None, :] >= starts[:, None]) & (token[None, :] < ends[:, None])).astype(F32)
    partial_cores = jnp.dot(member, outer, precision=lax.Precision.HIGHEST)
    cores = jnp.sum(lax.all_to_all(partial_cores, ("seq", "tensor"), 0, 0, tiled=True), axis=0)
    scaled = cores / eigen[0]
    terms = jnp.stack([jnp.sum(query_core[0] * scaled), jnp.sum(cores * scaled)])
    terms = jnp.sum(
        lax.all_to_all(jnp.broadcast_to(terms[None], (layers, 2)), "pipe", 0, 0, tiled=True), axis=0
    )
    return (terms[0] / jnp.sqrt(terms[1] + 1e-06)).reshape(1)


def solution(mesh):
    placed = (
        P("pipe", "seq", "tensor"),
        P("pipe", "tensor", "seq"),
        P("tensor", "seq"),
        P("tensor", "seq"),
        P("seq"),
        P("pipe", "seq", None),
        P("pipe", "tensor", None),
        P("pipe", None),
        P("pipe", None),
        P(),
    )
    return jax.shard_map(
        per_device, mesh=mesh, in_specs=placed, out_specs=P(("seq", "tensor")), check_vma=False
    )
```

time: 375 us -> 177 us (0.47)
  waiting for transfers between devices: 253 us -> 45.5 us
  blocking collectives: 81 us -> 22 us
  starting transfers between devices: 0.12 us -> 58.4 us
  Pallas kernels: 0 us -> 28.9 us
  matrix products: 21.7 us -> 2.22 us
  between operations: 15.1 us -> 2.29 us
  local copies, waits for them, and re-layouts: 0.71 us -> 8.73 us
  other arithmetic: 3.46 us -> 8.18 us
    unnamed x5 -> x0, waiting for transfers between devices: 138 us -> none
    all_gather x1 -> x0, waiting for transfers between devices: 90 us -> none  [per_device(): gathered = lax.all_gather(hidden[0], 'seq', axis=0, tiled=True)]
    psum x3 -> x0, blocking collectives: 81 us -> none  [the longest x1 50.4 us: per_device(): summed = lax.psum(partial_value, 'pipe')]
    all_to_all x0 -> x5, starting transfers between devices: none -> 35.4 us  [the longest x3 21.3 us: exchange(): lax.all_to_all(sent.reshape(peers, -1, width), ('tensor', 'pipe'), 0, 0)]
    pallas_call x0 -> x6, Pallas kernels: none -> 28.9 us  [the longest x4 25.7 us: product(): pl.pallas_call(functools.partial(product_kernel, len(pieces), len(extra)...]
    all_to_all x0 -> x5, waiting for transfers between devices: none -> 26.4 us  [the longest x3 16.9 us: exchange(): lax.all_to_all(sent.reshape(peers, -1, width), ('tensor', 'pipe'), 0, 0)]
    reduce_scatter x2 -> x0, waiting for transfers between devices: 24.7 us -> none  [the longest x1 24.6 us: per_device(): lax.psum_scatter(jnp.dot(gathered, weight, preferred_element_type=jnp.flo...]
    ppermute x0 -> x14, starting transfers between devices: none -> 23 us  [the longest x7 18.2 us: move(): lax.ppermute(pair[1], 'seq', down)]
  transfers between devices with their start and end apart: 4 -> 19, of which waited for: 3 -> 8; matrix products, arithmetic and copies ran while one was open for 2% -> 6% of each run, Pallas kernels for 0% -> 12%
where the time goes in v2:
time: 177 us; the launch traced here: 176 us
  starting transfers between devices  58.4 us (33%)
  waiting for transfers between devices  45.5 us (26%)
  Pallas kernels  28.9 us (16%)
  blocking collectives  22 us (12%)
  local copies, waits for them, and re-layouts  8.73 us (5%)
  other arithmetic  8.18 us (5%)
  between operations  2.29 us (1%)
  matrix products  2.22 us (1%)
    pallas_call x4, Pallas kernels, product(): pl.pallas_call(functools.partial(product_kernel, len(pieces), len(extra)...  25.7 us
    all_to_all x3, starting transfers between devices, exchange(): lax.all_to_all(sent.reshape(peers, -1, width), ('tensor', 'pipe'), 0, 0)  21.3 us
    ppermute x7, waiting for transfers between devices, move(): lax.ppermute(pair[0], 'seq', up)  19.1 us
    ppermute x7, starting transfers between devices, move(): lax.ppermute(pair[1], 'seq', down)  18.2 us
    all_to_all x3, waiting for transfers between devices, exchange(): lax.all_to_all(sent.reshape(peers, -1, width), ('tensor', 'pipe'), 0, 0)  16.9 us
    all_to_all x1, blocking collectives, per_device(): lax.all_to_all(partial_cores, ('seq', 'tensor'), 0, 0, tiled=True)  12.6 us
    all_to_all x1, waiting for transfers between devices, per_device(): packed = lax.all_to_all(packed, ('pipe', 'seq'), 0, 0)  9.46 us
    all_to_all x1, blocking collectives, per_device(): lax.all_to_all(jnp.broadcast_to(terms[None], (layers, 2)), 'pipe', 0, 0,...  9.44 us
  transfers between devices with their start and end apart: 19, of which 8 were waited for; matrix products, arithmetic and copies ran while one was open for 6% of the time, Pallas kernels for 12%

profile of v2, /device:TPU:1, one launch (start us, length us, event | category | flops | bytes accessed | tf_op | source)
XLA Modules:
  0.0 176.3 jit_solution(14674788988043721760)
XLA Ops:
  2.2 2.5 %collective-permute-start = (bf16[64,3584]{1,0:T(8,128)(2,1)}, bf16[64,3584]{1,0:T(8,128)(2,1)}, u32[]{:S(2)}, u32[]{:S(2)}) collective-permute-start(bf16[64,3584]{1,0:T(8,128)(2,1)} %get-tuple-element.40), channel_id=1, source_target_pairs={{0,4},{4,8},{8,12},{12,16},{16,20},{20,24},{24,28},{28,0},{1,5},{5... | collective-permute-start | bytes 1376264 | tf_op jit(solution)/shard_map/ppermute | solution.py:176
  4.7 3.9 %collective-permute-start.1 = (bf16[64,3584]{1,0:T(8,128)(2,1)}, bf16[64,3584]{1,0:T(8,128)(2,1)}, u32[]{:S(2)}, u32[]{:S(2)}) collective-permute-start(bf16[64,3584]{1,0:T(8,128)(2,1)} %get-tuple-element.39), channel_id=1, source_target_pairs={{0,28},{4,0},{8,4},{12,8},{16,12},{20,16},{24,20},{28,24},{1,29},{... | collective-permute-start | bytes 1376264 | tf_op jit(solution)/shard_map/ppermute | solution.py:176
  10.6 2.7 %collective-permute-start.5 = (bf16[64,3584]{1,0:T(8,128)(2,1)}, bf16[64,3584]{1,0:T(8,128)(2,1)}, u32[]{:S(2)}, u32[]{:S(2)}) collective-permute-start(bf16[64,3584]{1,0:T(8,128)(2,1)} %get-tuple-element.40), channel_id=1, source_target_pairs={{0,28},{4,0},{8,4},{12,8},{16,12},{20,16},{24,20},{28,24},{1,29},{... | collective-permute-start | bytes 1376264 | tf_op jit(solution)/shard_map/ppermute | solution.py:176
  13.3 5.8 %all-to-all-start = ((f32[8,32,1024]{2,1,0:T(8,128)}), f32[8,32,1024]{2,1,0:T(8,128)S(1)}, u32[]{:S(2)}, u32[]{:S(2)}) async-start(f32[8,32,1024]{2,1,0:T(8,128)} %broadcast_in_dim.88), calls=%async_computation | async-start | bytes 2097152 | tf_op jit(solution)/shard_map/all_to_all | solution.py:204
  23.1 2.7 %collective-permute-start.3 = (bf16[64,3584]{1,0:T(8,128)(2,1)}, bf16[64,3584]{1,0:T(8,128)(2,1)}, u32[]{:S(2)}, u32[]{:S(2)}) collective-permute-start(bf16[64,3584]{1,0:T(8,128)(2,1)} %collective-permute-done.1.refs_2_), channel_id=1, source_target_pairs={{0,28},{4,0},{8,4},{12,8},{16,12},{20,16},{24,20},{28,24},{1,29},{... | collective-permute-start | bytes 1376264 | tf_op jit(solution)/shard_map/ppermute | solution.py:176
  26.2 2.7 %collective-permute-done.4.refs_4_ = bf16[64,3584]{1,0:T(8,128)(2,1)} collective-permute-done((bf16[64,3584]{1,0:T(8,128)(2,1)}, bf16[64,3584]{1,0:T(8,128)(2,1)}, u32[]{:S(2)}, u32[]{:S(2)}) %collective-permute-start.4) | collective-permute-done | bytes 458784 | tf_op jit(solution)/shard_map/ppermute | solution.py:176
  29.9 8.5 %shard_map.100 = bf16[512,1024]{1,0:T(8,128)(2,1)} custom-call(bf16[128,3584]{1,0:T(8,128)(2,1)S(1)} %bitcast.40, bf16[64,3584]{1,0:T(8,128)(2,1)} %collective-permute-done.refs_1_, bf16[64,3584]{1,0:T(8,128)(2,1)} %collective-permute-done.1.refs_2_, bf16[64,3584]{1,0:T(8,128)(2,1)} %collective-permute-done.5.refs_3_, ...), custom_call_target="tpu_custom_call" | custom-call | flops 1048576 | bytes 65536 | tf_op jit(solution)/shard_map/pallas_call | solution.py:73
  38.8 8.9 %all-to-all-start.1 = ((bf16[32,16,1024]{2,1,0:T(8,128)(2,1)}), bf16[32,16,1024]{2,1,0:T(8,128)(2,1)}, u32[]{:S(2)}, u32[]{:S(2)}) async-start(bf16[32,16,1024]{2,1,0:T(8,128)(2,1)} %bitcast.9), calls=%async_computation.1 | async-start | bytes 2097152 | tf_op jit(solution)/shard_map/all_to_all | solution.py:195
  47.8 3.1 %collective-permute-start.8 = (bf16[64,3584]{1,0:T(8,128)(2,1)}, bf16[64,3584]{1,0:T(8,128)(2,1)S(1)}, u32[]{:S(2)}, u32[]{:S(2)}) collective-permute-start(bf16[64,3584]{1,0:T(8,128)(2,1)} %collective-permute-done.5.refs_3_), channel_id=1, source_target_pairs={{0,28},{4,0},{8,4},{12,8},{16,12},{20,16},{24,20},{28,24},{1,29},{... | collective-permute-start | bytes 1376264 | tf_op jit(solution)/shard_map/ppermute | solution.py:176
  50.9 2.7 %collective-permute-start.7 = (bf16[64,3584]{1,0:T(8,128)(2,1)}, bf16[64,3584]{1,0:T(8,128)(2,1)}, u32[]{:S(2)}, u32[]{:S(2)}) collective-permute-start(bf16[64,3584]{1,0:T(8,128)(2,1)} %collective-permute-done.3.refs_1_), channel_id=1, source_target_pairs={{0,28},{4,0},{8,4},{12,8},{16,12},{20,16},{24,20},{28,24},{1,29},{... | collective-permute-start | bytes 1376264 | tf_op jit(solution)/shard_map/ppermute | solution.py:176
  53.5 8.2 %collective-permute-done.9.refs_3_ = bf16[64,3584]{1,0:T(8,128)(2,1)S(1)} collective-permute-done((bf16[64,3584]{1,0:T(8,128)(2,1)}, bf16[64,3584]{1,0:T(8,128)(2,1)S(1)}, u32[]{:S(2)}, u32[]{:S(2)}) %collective-permute-start.9) | collective-permute-done | bytes 458784 | tf_op jit(solution)/shard_map/ppermute | solution.py:176
  61.7 2.7 %collective-permute-start.13 = (bf16[64,3584]{1,0:T(8,128)(2,1)S(1)}, bf16[64,3584]{1,0:T(8,128)(2,1)}, u32[]{:S(2)}, u32[]{:S(2)}) collective-permute-start(bf16[64,3584]{1,0:T(8,128)(2,1)S(1)} %collective-permute-done.8.refs_2_), channel_id=1, source_target_pairs={{0,28},{4,0},{8,4},{12,8},{16,12},{20,16},{24,20},{28,24},{1,29},{... | collective-permute-start | bytes 1376264 | tf_op jit(solution)/shard_map/ppermute | solution.py:176
  65.5 5.4 %shard_map.101 = bf16[256,1024]{1,0:T(8,128)(2,1)} custom-call(bf16[64,3584]{1,0:T(8,128)(2,1)} %collective-permute-done.2.refs_0_, bf16[64,3584]{1,0:T(8,128)(2,1)} %collective-permute-done.3.refs_1_, bf16[64,3584]{1,0:T(8,128)(2,1)S(1)} %collective-permute-done.8.refs_2_, bf16[64,3584]{1,0:T(8,128)(2,1)S(1)} %collective-permute-done.9.refs_3_, ...), custom_call_target="tpu_custom_call" | custom-call | flops 1048576 | bytes 65536 | tf_op jit(solution)/shard_map/pallas_call | solution.py:73
  74.3 7.1 %collective-permute-done.12.refs_3_ = bf16[64,3584]{1,0:T(8,128)(2,1)} collective-permute-done((bf16[64,3584]{1,0:T(8,128)(2,1)S(1)}, bf16[64,3584]{1,0:T(8,128)(2,1)}, u32[]{:S(2)}, u32[]{:S(2)}) %collective-permute-start.12) | collective-permute-done | bytes 458784 | tf_op jit(solution)/shard_map/ppermute | solution.py:176
  81.4 8.4 %all-to-all-start.2 = ((bf16[32,8,1024]{2,1,0:T(8,128)(2,1)}), bf16[32,8,1024]{2,1,0:T(8,128)(2,1)}, u32[]{:S(2)}, u32[]{:S(2)}) async-start(bf16[32,8,1024]{2,1,0:T(8,128)(2,1)} %bitcast.10), calls=%async_computation.2 | async-start | bytes 1048576 | tf_op jit(solution)/shard_map/all_to_all | solution.py:195
  91.1 6.2 %shard_map.102.refs_4_ = bf16[512,1024]{1,0:T(8,128)(2,1)S(1)} custom-call(bf16[64,3584]{1,0:T(8,128)(2,1)} %collective-permute-done.6.refs_0_, bf16[64,3584]{1,0:T(8,128)(2,1)} %collective-permute-done.7.refs_1_, bf16[64,3584]{1,0:T(8,128)(2,1)} %collective-permute-done.13.refs_2_, bf16[64,3584]{1,0:T(8,128)(2,1)} %collective-permute-done.12.refs_3_, ...), custom_call_target="tpu_custom_call" | custom-call | flops 1048576 | bytes 65536 | tf_op jit(solution)/shard_map/pallas_call | solution.py:73
  97.3 4.1 %all-to-all-done.2 = bf16[32,8,1024]{2,1,0:T(8,128)(2,1)} async-done(((bf16[32,8,1024]{2,1,0:T(8,128)(2,1)}), bf16[32,8,1024]{2,1,0:T(8,128)(2,1)}, u32[]{:S(2)}, u32[]{:S(2)}) %all-to-all-start.2) | async-done | bytes 524320 | tf_op jit(solution)/shard_map/all_to_all | solution.py:195
  101.4 5.6 %shard_map.103 = bf16[512,1024]{1,0:T(8,128)(2,1)} custom-call(bf16[64,3584]{1,0:T(8,128)(2,1)} %collective-permute-done.10.refs_0_, bf16[64,3584]{1,0:T(8,128)(2,1)} %collective-permute-done.11.refs_1_, bf16[3584,1024]{1,0:T(8,128)(2,1)} %bitcast.44, bf16[512,128]{1,0:T(8,128)(2,1)S(1)} %get-tuple-element.62.refs_3_, bf16[512,1024]{1,0:T(8,128)(2,1)S(1)} %shard_map.102.refs_4_), custom_call_target="tpu_custom_call" | custom-call | flops 1048576 | bytes 65536 | tf_op jit(solution)/shard_map/pallas_call | solution.py:73
  107.0 4.0 %all-to-all-start.3 = ((bf16[32,16,1024]{2,1,0:T(8,128)(2,1)}), bf16[32,16,1024]{2,1,0:T(8,128)(2,1)S(1)}, u32[]{:S(2)}, u32[]{:S(2)}) async-start(bf16[32,16,1024]{2,1,0:T(8,128)(2,1)} %bitcast.11), calls=%async_computation.3 | async-start | bytes 2097152 | tf_op jit(solution)/shard_map/all_to_all | solution.py:195
  115.4 12.9 %all-to-all-done.3.got = bf16[32,16,1024]{2,1,0:T(8,128)(2,1)S(1)} async-done(((bf16[32,16,1024]{2,1,0:T(8,128)(2,1)}), bf16[32,16,1024]{2,1,0:T(8,128)(2,1)S(1)}, u32[]{:S(2)}, u32[]{:S(2)}) %all-to-all-start.3) | async-done | bytes 1048608 | tf_op jit(solution)/shard_map/all_to_all | solution.py:195
  130.3 8.3 %all-to-all-start.4 = ((f32[64,1,384]{2,1,0:T(1,128)}), f32[64,1,384]{2,1,0:T(1,128)S(1)}, u32[]{:S(2)}, u32[]{:S(2)}) async-start(f32[64,1,384]{2,1,0:T(1,128)} %shard_map.105), calls=%async_computation.4 | async-start | bytes 196608 | tf_op jit(solution)/shard_map/all_to_all | solution.py:292
  138.9 9.5 %all-to-all-done.4 = f32[64,1,384]{2,1,0:T(1,128)S(1)} async-done(((f32[64,1,384]{2,1,0:T(1,128)}), f32[64,1,384]{2,1,0:T(1,128)S(1)}, u32[]{:S(2)}, u32[]{:S(2)}) %all-to-all-start.4) | async-done | bytes 98336 | tf_op jit(solution)/shard_map/all_to_all | solution.py:292
  149.7 12.6 %all_to_all.40 = f32[32,1,1024]{2,1,0:T(1,128)S(1)} all-to-all(f32[32,1,1024]{2,1,0:T(1,128)S(1)} %copy.18), channel_id=1, replica_groups=mesh['pipe'=8,'seq'=8,'tensor'=4] {'seq','tensor'}, dimensions={0} | all-to-all | bytes 262144 | tf_op jit(solution)/shard_map/all_to_all | solution.py:309
  164.4 9.4 %all_to_all.41 = f32[8,1,2]{2,1,0:T(1,128)S(1)} all-to-all(f32[8,1,2]{2,1,0:T(1,128)S(1)} %broadcast_in_dim.96), channel_id=1, replica_groups=mesh['pipe'=8,'seq'=8,'tensor'=4] {'pipe'}, dimensions={0} | all-to-all | bytes 128 | tf_op jit(solution)/shard_map/all_to_all | solution.py:313
  (96 shorter events, 26.3 us)
Async XLA Ops:
  0.0 25.7 %copy-start = (bf16[1,3584,32]{1,2,0:T(8,128)(2,1)S(1)}, bf16[1,3584,32]{1,2,0:T(8,128)(2,1)}, u32[]{:S(2)}) copy-start(bf16[1,3584,32]{1,2,0:T(8,128)(2,1)} %param.16) | copy-start | bytes 688132
  2.2 20.8 %collective-permute-start = (bf16[64,3584]{1,0:T(8,128)(2,1)}, bf16[64,3584]{1,0:T(8,128)(2,1)}, u32[]{:S(2)}, u32[]{:S(2)}) collective-permute-start(bf16[64,3584]{1,0:T(8,128)(2,1)} %get-tuple-element.40), channel_id=1, source_target_pairs={{0,4},{4,8},{8,12},{12,16},{16,20},{20,24},{24,28},{28,0},{1,5},{5... | collective-permute-start | bytes 1376264 | tf_op jit(solution)/shard_map/ppermute | solution.py:176
  4.7 18.3 %collective-permute-start.1 = (bf16[64,3584]{1,0:T(8,128)(2,1)}, bf16[64,3584]{1,0:T(8,128)(2,1)}, u32[]{:S(2)}, u32[]{:S(2)}) collective-permute-start(bf16[64,3584]{1,0:T(8,128)(2,1)} %get-tuple-element.39), channel_id=1, source_target_pairs={{0,28},{4,0},{8,4},{12,8},{16,12},{20,16},{24,20},{28,24},{1,29},{... | collective-permute-start | bytes 1376264 | tf_op jit(solution)/shard_map/ppermute | solution.py:176
  10.6 18.4 %collective-permute-start.4 = (bf16[64,3584]{1,0:T(8,128)(2,1)}, bf16[64,3584]{1,0:T(8,128)(2,1)}, u32[]{:S(2)}, u32[]{:S(2)}) collective-permute-start(bf16[64,3584]{1,0:T(8,128)(2,1)} %get-tuple-element.39), channel_id=1, source_target_pairs={{0,4},{4,8},{8,12},{12,16},{16,20},{20,24},{24,28},{28,0},{1,5},{5... | collective-permute-start | bytes 1376264 | tf_op jit(solution)/shard_map/ppermute | solution.py:176
  10.6 18.4 %collective-permute-start.5 = (bf16[64,3584]{1,0:T(8,128)(2,1)}, bf16[64,3584]{1,0:T(8,128)(2,1)}, u32[]{:S(2)}, u32[]{:S(2)}) collective-permute-start(bf16[64,3584]{1,0:T(8,128)(2,1)} %get-tuple-element.40), channel_id=1, source_target_pairs={{0,28},{4,0},{8,4},{12,8},{16,12},{20,16},{24,20},{28,24},{1,29},{... | collective-permute-start | bytes 1376264 | tf_op jit(solution)/shard_map/ppermute | solution.py:176
  13.3 25.5 %all-to-all-start = ((f32[8,32,1024]{2,1,0:T(8,128)}), f32[8,32,1024]{2,1,0:T(8,128)S(1)}, u32[]{:S(2)}, u32[]{:S(2)}) async-start(f32[8,32,1024]{2,1,0:T(8,128)} %broadcast_in_dim.88), calls=%async_computation | async-start | bytes 2097152 | tf_op jit(solution)/shard_map/all_to_all | solution.py:204
  23.0 15.8 %collective-permute-start.2 = (bf16[64,3584]{1,0:T(8,128)(2,1)}, bf16[64,3584]{1,0:T(8,128)(2,1)}, u32[]{:S(2)}, u32[]{:S(2)}) collective-permute-start(bf16[64,3584]{1,0:T(8,128)(2,1)} %collective-permute-done.refs_1_), channel_id=1, source_target_pairs={{0,4},{4,8},{8,12},{12,16},{16,20},{20,24},{24,28},{28,0},{1,5},{5... | collective-permute-start | bytes 1376264 | tf_op jit(solution)/shard_map/ppermute | solution.py:176
  23.1 15.8 %collective-permute-start.3 = (bf16[64,3584]{1,0:T(8,128)(2,1)}, bf16[64,3584]{1,0:T(8,128)(2,1)}, u32[]{:S(2)}, u32[]{:S(2)}) collective-permute-start(bf16[64,3584]{1,0:T(8,128)(2,1)} %collective-permute-done.1.refs_2_), channel_id=1, source_target_pairs={{0,28},{4,0},{8,4},{12,8},{16,12},{20,16},{24,20},{28,24},{1,29},{... | collective-permute-start | bytes 1376264 | tf_op jit(solution)/shard_map/ppermute | solution.py:176
  29.9 34.5 %copy-start.8 = (s32[32]{0:T(128)S(1)}, s32[32]{0:T(128)}, u32[]{:S(2)}) copy-start(s32[32]{0:T(128)} %param.19) | copy-start | bytes 388
  38.8 42.6 %all-to-all-start.1 = ((bf16[32,16,1024]{2,1,0:T(8,128)(2,1)}), bf16[32,16,1024]{2,1,0:T(8,128)(2,1)}, u32[]{:S(2)}, u32[]{:S(2)}) async-start(bf16[32,16,1024]{2,1,0:T(8,128)(2,1)} %bitcast.9), calls=%async_computation.1 | async-start | bytes 2097152 | tf_op jit(solution)/shard_map/all_to_all | solution.py:195
  47.7 14.0 %collective-permute-start.9 = (bf16[64,3584]{1,0:T(8,128)(2,1)}, bf16[64,3584]{1,0:T(8,128)(2,1)S(1)}, u32[]{:S(2)}, u32[]{:S(2)}) collective-permute-start(bf16[64,3584]{1,0:T(8,128)(2,1)} %collective-permute-done.4.refs_4_), channel_id=1, source_target_pairs={{0,4},{4,8},{8,12},{12,16},{16,20},{20,24},{24,28},{28,0},{1,5},{5... | collective-permute-start | bytes 1376264 | tf_op jit(solution)/shard_map/ppermute | solution.py:176
  47.8 14.0 %collective-permute-start.8 = (bf16[64,3584]{1,0:T(8,128)(2,1)}, bf16[64,3584]{1,0:T(8,128)(2,1)S(1)}, u32[]{:S(2)}, u32[]{:S(2)}) collective-permute-start(bf16[64,3584]{1,0:T(8,128)(2,1)} %collective-permute-done.5.refs_3_), channel_id=1, source_target_pairs={{0,28},{4,0},{8,4},{12,8},{16,12},{20,16},{24,20},{28,24},{1,29},{... | collective-permute-start | bytes 1376264 | tf_op jit(solution)/shard_map/ppermute | solution.py:176
  50.9 20.7 %collective-permute-start.6 = (bf16[64,3584]{1,0:T(8,128)(2,1)}, bf16[64,3584]{1,0:T(8,128)(2,1)}, u32[]{:S(2)}, u32[]{:S(2)}) collective-permute-start(bf16[64,3584]{1,0:T(8,128)(2,1)} %collective-permute-done.2.refs_0_), channel_id=1, source_target_pairs={{0,4},{4,8},{8,12},{12,16},{16,20},{20,24},{24,28},{28,0},{1,5},{5... | collective-permute-start | bytes 1376264 | tf_op jit(solution)/shard_map/ppermute | solution.py:176
  50.9 20.7 %collective-permute-start.7 = (bf16[64,3584]{1,0:T(8,128)(2,1)}, bf16[64,3584]{1,0:T(8,128)(2,1)}, u32[]{:S(2)}, u32[]{:S(2)}) collective-permute-start(bf16[64,3584]{1,0:T(8,128)(2,1)} %collective-permute-done.3.refs_1_), channel_id=1, source_target_pairs={{0,28},{4,0},{8,4},{12,8},{16,12},{20,16},{24,20},{28,24},{1,29},{... | collective-permute-start | bytes 1376264 | tf_op jit(solution)/shard_map/ppermute | solution.py:176
  61.7 19.7 %collective-permute-start.12 = (bf16[64,3584]{1,0:T(8,128)(2,1)S(1)}, bf16[64,3584]{1,0:T(8,128)(2,1)}, u32[]{:S(2)}, u32[]{:S(2)}) collective-permute-start(bf16[64,3584]{1,0:T(8,128)(2,1)S(1)} %collective-permute-done.9.refs_3_), channel_id=1, source_target_pairs={{0,4},{4,8},{8,12},{12,16},{16,20},{20,24},{24,28},{28,0},{1,5},{5... | collective-permute-start | bytes 1376264 | tf_op jit(solution)/shard_map/ppermute | solution.py:176
  61.7 19.7 %collective-permute-start.13 = (bf16[64,3584]{1,0:T(8,128)(2,1)S(1)}, bf16[64,3584]{1,0:T(8,128)(2,1)}, u32[]{:S(2)}, u32[]{:S(2)}) collective-permute-start(bf16[64,3584]{1,0:T(8,128)(2,1)S(1)} %collective-permute-done.8.refs_2_), channel_id=1, source_target_pairs={{0,28},{4,0},{8,4},{12,8},{16,12},{20,16},{24,20},{28,24},{1,29},{... | collective-permute-start | bytes 1376264 | tf_op jit(solution)/shard_map/ppermute | solution.py:176
  65.4 25.6 %copy-start.2 = (bf16[512,128]{1,0:T(8,128)(2,1)S(1)}, bf16[512,128]{1,0:T(8,128)(2,1)}, u32[]{:S(2)}) copy-start(bf16[512,128]{1,0:T(8,128)(2,1)} %fusion.8.refs_6_) | copy-start | bytes 393220
  71.6 25.7 %collective-permute-start.10 = (bf16[64,3584]{1,0:T(8,128)(2,1)}, bf16[64,3584]{1,0:T(8,128)(2,1)}, u32[]{:S(2)}, u32[]{:S(2)}) collective-permute-start(bf16[64,3584]{1,0:T(8,128)(2,1)} %collective-permute-done.6.refs_0_), channel_id=1, source_target_pairs={{0,4},{4,8},{8,12},{12,16},{16,20},{20,24},{24,28},{28,0},{1,5},{5... | collective-permute-start | bytes 1376264 | tf_op jit(solution)/shard_map/ppermute | solution.py:176
  73.8 23.6 %collective-permute-start.11 = (bf16[64,3584]{1,0:T(8,128)(2,1)}, bf16[64,3584]{1,0:T(8,128)(2,1)}, u32[]{:S(2)}, u32[]{:S(2)}) collective-permute-start(bf16[64,3584]{1,0:T(8,128)(2,1)} %collective-permute-done.7.refs_1_), channel_id=1, source_target_pairs={{0,28},{4,0},{8,4},{12,8},{16,12},{20,16},{24,20},{28,24},{1,29},{... | collective-permute-start | bytes 1376264 | tf_op jit(solution)/shard_map/ppermute | solution.py:176
  81.4 20.0 %all-to-all-start.2 = ((bf16[32,8,1024]{2,1,0:T(8,128)(2,1)}), bf16[32,8,1024]{2,1,0:T(8,128)(2,1)}, u32[]{:S(2)}, u32[]{:S(2)}) async-start(bf16[32,8,1024]{2,1,0:T(8,128)(2,1)} %bitcast.10), calls=%async_computation.2 | async-start | bytes 1048576 | tf_op jit(solution)/shard_map/all_to_all | solution.py:195
  107.0 21.3 %all-to-all-start.3 = ((bf16[32,16,1024]{2,1,0:T(8,128)(2,1)}), bf16[32,16,1024]{2,1,0:T(8,128)(2,1)S(1)}, u32[]{:S(2)}, u32[]{:S(2)}) async-start(bf16[32,16,1024]{2,1,0:T(8,128)(2,1)} %bitcast.11), calls=%async_computation.3 | async-start | bytes 2097152 | tf_op jit(solution)/shard_map/all_to_all | solution.py:195
  115.4 47.0 %copy-start.6 = (f32[1,1024]{1,0:T(1,128)S(1)}, f32[1,1024]{1,0:T(1,128)}, u32[]{:S(2)}) copy-start(f32[1,1024]{1,0:T(1,128)} %param.17) | copy-start | bytes 12292
  115.4 47.0 %copy-start.7 = (f32[1,1024]{1,0:T(1,128)S(1)}, f32[1,1024]{1,0:T(1,128)}, u32[]{:S(2)}) copy-start(f32[1,1024]{1,0:T(1,128)} %param.18) | copy-start | bytes 12292
  130.3 18.0 %all-to-all-start.4 = ((f32[64,1,384]{2,1,0:T(1,128)}), f32[64,1,384]{2,1,0:T(1,128)S(1)}, u32[]{:S(2)}, u32[]{:S(2)}) async-start(f32[64,1,384]{2,1,0:T(1,128)} %shard_map.105), calls=%async_computation.4 | async-start | bytes 196608 | tf_op jit(solution)/shard_map/all_to_all | solution.py:292
  (4 other events, 39.3 us)

commit v3 on v2

--- a/solution.py
+++ b/solution.py
@@ -13,6 +13,8 @@
 VMEM_BYTES = 16 << 20
 PRODUCT_BYTES = 28 << 20
 TILES = 4
+CHUNK = 256
+FLOPS_PER_MICRO = 1_150_000_000
 
 
 def exact_dot(a, b, dims):
@@ -25,7 +27,7 @@
     pieces, weight, order, refs = refs[:count], refs[count], refs[count + 1], refs[count + 2 :]
     extra, refs = refs[: 2 * extras], refs[2 * extras :]
     base, refs = (refs[0], refs[1:]) if based else (None, refs)
-    out, rows, tiles, total, sems, tile_sems = refs
+    out, rows, tiles, sums, result, start, sems, tile_sems, out_sems, base_sem = refs
     depth = tiles.shape[1]
 
     def fetch(k):
@@ -43,6 +45,9 @@
         copy.start()
     for k in range(1, TILES):
         fetch(k).start()
+    if based:
+        first_rows = pltpu.make_async_copy(base, start, base_sem)
+        first_rows.start()
     for copy in copies:
         copy.wait()
     for k in range(TILES):
@@ -51,40 +56,61 @@
             rows[:, k * depth : (k + 1) * depth], tiles[k], preferred_element_type=F32
         )
         if k == 0:
-            total[...] = value
+            sums[...] = value
         elif k < TILES - 1:
-            total[...] += value
-    value = (total[...] + value).astype(BF16)
-    value = jnp.dot(order[...], value, preferred_element_type=F32)
-    for k in range(extras):
-        value += jnp.dot(extra[2 * k][...], extra[2 * k + 1][...], preferred_element_type=F32)
+            sums[...] += value
+    value = (sums[...] + value).astype(BF16)
     if based:
-        value += base[...].astype(F32)
-    out[...] = value.astype(BF16)
-
-
-def product(pieces, weight, order, extra=(), base=None):
+        first_rows.wait()
+    stores = []
+    for k in range(out.shape[0] // CHUNK):
+        cut = pl.ds(k * CHUNK, CHUNK)
+        part = jnp.dot(order[cut, :], value, preferred_element_type=F32)
+        for m in range(extras):
+            part += jnp.dot(
+                extra[2 * m][cut, :], extra[2 * m + 1][...], preferred_element_type=F32
+            )
+        if based:
+            part += start[cut, :].astype(F32)
+        result[cut, :] = part.astype(BF16)
+        stores.append(pltpu.make_async_copy(result.at[cut], out.at[cut], out_sems.at[k]))
+        stores[-1].start()
+    for store in stores:
+        store.wait()
+
+
+def product(micros, pieces, weight, order, extra=(), base=None):
     total = sum(p.shape[0] for p in pieces)
     depth, width = weight.shape
     height = order.shape[0]
-    anywhere, held = pl.BlockSpec(memory_space=pl.ANY), pl.BlockSpec(memory_space=pltpu.VMEM)
+    based = base is not None
+    anywhere, held = pl.BlockSpec(memory_space=pltpu.HBM), pl.BlockSpec(memory_space=pltpu.VMEM)
+    far = pltpu.with_memory_space_constraint
     weight = pltpu.with_memory_space_constraint(weight, pltpu.HBM)
-    small = [order, *extra] + ([] if base is None else [base])
+    pieces = [far(p, pltpu.HBM) for p in pieces]
+    bases = [far(base, pltpu.HBM)] if based else []
+    small = [order, *extra]
     return pl.pallas_call(
-        functools.partial(product_kernel, len(pieces), len(extra) // 2, base is not None),
-        out_shape=jax.ShapeDtypeStruct((height, width), BF16),
-        in_specs=[anywhere] * len(pieces) + [pl.BlockSpec(memory_space=pltpu.HBM)] + [held] * len(small),
-        out_specs=held,
+        functools.partial(product_kernel, len(pieces), len(extra) // 2, based),
+        out_shape=pltpu.HBM((height, width), BF16),
+        in_specs=[anywhere] * len(pieces) + [pl.BlockSpec(memory_space=pltpu.HBM)] + [held] * len(small) + [anywhere] * len(bases),
+        out_specs=anywhere,
         scratch_shapes=[
             pltpu.VMEM((total, depth), BF16),
             pltpu.VMEM((TILES, depth // TILES, width), BF16),
             pltpu.VMEM((total, width), F32),
+            pltpu.VMEM((height, width), BF16),
+            pltpu.VMEM((height if based else CHUNK, width), BF16),
             pltpu.SemaphoreType.DMA((len(pieces),)),
             pltpu.SemaphoreType.DMA((TILES,)),
+            pltpu.SemaphoreType.DMA((height // CHUNK,)),
+            pltpu.SemaphoreType.DMA,
         ],
         compiler_params=pltpu.CompilerParams(vmem_limit_bytes=PRODUCT_BYTES),
-        cost_estimate=pl.CostEstimate(flops=1 << 20, bytes_accessed=1 << 16, transcendentals=0),
-    )(*pieces, weight, *small)
+        cost_estimate=pl.CostEstimate(
+            flops=micros * FLOPS_PER_MICRO, bytes_accessed=1 << 16, transcendentals=0
+        ),
+    )(*pieces, weight, *small, *bases)
 
 
 def reduce_rows(got, resid, aim, left, height):
@@ -212,44 +238,46 @@
     right_rows = jnp.concatenate([right_high.astype(BF16), right_low], axis=0)
     right_rows = jnp.pad(right_rows, ((0, 128 - 2 * tensors), (0, 0)))
 
-    near = 3
-    peer, slot, line = layout(near + 1)
-    spare = (slot == near) & (line < 2)
+    near, far = 6, 4
+    peer, slot, line = layout(near)
+    spare = slot == near - 1
     aside_order = one_hot(
-        jnp.where(spare, peer * share + layer % 2 * 2 + line, -1), block_rows
+        jnp.where(spare & (line < 2), peer * share + layer % 2 * 2 + line, -1), block_rows
     )
     right_order = one_hot(
-        jnp.where(spare & (peer % layers == layer), line * tensors + peer // layers, -1), 128
-    )
-    near_order, middle_order = units(near + 1, 0, 3), units(2, 0, 2)
-    pair_order, last_order = units(near + 1, 0, 2), units(near + 1, 2, 1)
-    near_order, middle_order, pair_order, last_order, aside_order, right_order, a1, aside = tie(
-        (near_order, middle_order, pair_order, last_order, aside_order, right_order, a1, aside)
-    )
+        jnp.where(
+            spare & (line >= 2) & (peer % layers == layer),
+            (line - 2) * tensors + peer // layers,
+            -1,
+        ),
+        128,
+    )
+    orders = units(near, 0, 3), units(near, 3, 2), units(far, 0, 2), units(far, 2, 1)
+    orders, aside_order, right_order, a1, aside = tie((orders, aside_order, right_order, a1, aside))
 
     a2 = move(a1)
     b1, right_rows = tie((b1, right_rows))
     b2 = move(b1)
-    sent = product(
-        [own, a1[0], a1[1], b1[1], b1[0]], weight, near_order, (aside_order, aside)
+    sent = product(1,
+        [own, a1[0], a1[1], b1[1], b1[0]], weight, orders[0], (aside_order, aside)
     )
     a2, sent, left_all = tie((a2, sent, left_all))
-    got_near = exchange(sent)
     a3 = move(a2)
     b3 = move(b2)
-    sent = product([a2[0], a2[1], b2[1], b2[0]], weight, middle_order)
+    sent = product(6,
+        [a2[0], a2[1], b2[1], b2[0]], weight, orders[1], (right_order, right_rows), base=sent
+    )
+    got_near = exchange(sent)
     a3, sent = tie((a3, sent))
     a4 = move(a3)
-    b3, sent, got_near = tie((b3, sent, got_near))
-    got_middle = exchange(sent)
-    sent = product(
-        [a3[0], a3[1], b3[1], b3[0]], weight, pair_order, (right_order, right_rows)
-    )
-    a4, sent, got_middle = tie((a4, sent, got_middle))
-    got_far = exchange(product(list(a4), weight, last_order, base=sent))
+    sent = product(6, [a3[0], a3[1], b3[1], b3[0]], weight, orders[2])
+    a4, sent = tie((a4, sent))
+    sent = product(6, list(a4), weight, orders[3], base=sent)
+    sent, got_near = tie((sent, got_near))
+    got_far = exchange(sent)
 
     turned = jnp.where(tensor < tensors // 2, 1, -1)
-    slots = [0, -1, 1, None, -2, 2, -3, 3, seqs // 2, None]
+    slots = [0, -1, 1, -2, 2, None, -3, 3, seqs // 2, None]
     slot = column(len(slots) * share)
     offset = jnp.zeros_like(slot)
     filled = jnp.ones_like(slot)
@@ -264,18 +292,17 @@
     by_line = jnp.where(filled == 1, slot % share * seqs + block, -1)
     order = (column(seqs * share)[:, None] == by_line[None, :]).astype(F32)
 
-    both = got_near[:, near * share : near * share + 2].reshape(
+    cut = near * share
+    both = got_near[:, cut - share : cut - share + 2].reshape(
         tensors, 2, local_blocks * share, width
     )
     both = jnp.transpose(both, (1, 0, 2, 3)).reshape(2, seqs * share, width)
     turn = turn.astype(BF16)
     resid_rows = jnp.dot(turn, both[0], preferred_element_type=F32)
     aim_rows = gain[None, :] * jnp.dot(turn, both[1], preferred_element_type=F32)
-    right_proj = jnp.sum(got_far[:, near * share : near * share + 2].astype(F32), axis=(0, 1))
+    right_proj = jnp.sum(got_near[:, cut - share + 2 :].astype(F32), axis=(0, 1))
     right_proj = right_proj.reshape(strip, rank)
-    got_first = jnp.concatenate([got_near, got_middle], axis=1)
-    cut = got_first.shape[1]
-    first = stats(got_first, resid_rows[:cut], aim_rows[:cut], left_all)
+    first = stats(got_near, resid_rows[:cut], aim_rows[:cut], left_all)
     target_proj = exact_dot(order, exact_dot(aim_rows, left_all, ((1,), (1,))), ((1,), (0,)))
     packed = pack(
         layers,

time: 177 us -> 165 us (0.932)
  waiting for transfers between devices: 45.5 us -> 37.5 us
  Pallas kernels: 28.9 us -> 33.4 us
  starting transfers between devices: 58.4 us -> 54.4 us
  other arithmetic: 8.18 us -> 5.5 us
    ppermute x7, waiting for transfers between devices: 19.1 us -> 8.69 us  [move(): lax.ppermute(pair[0], 'seq', up)]
    all_to_all x3 -> x2, starting transfers between devices: 21.3 us -> 16.9 us  [exchange(): lax.all_to_all(sent.reshape(peers, -1, width), ('tensor', 'pipe'), 0, 0)]
    ppermute x7, waiting for transfers between devices: 0.02 us -> 4.34 us  [move(): lax.ppermute(pair[1], 'seq', down)]
    pallas_call x4, Pallas kernels: 25.7 us -> 28.9 us  [product(): pl.pallas_call(functools.partial(product_kernel, len(pieces), len(extra)...]
    ppermute x7, starting transfers between devices: 18.2 us -> 20.8 us  [move(): lax.ppermute(pair[1], 'seq', down)]
    ppermute x7, starting transfers between devices: 4.82 us -> 2.73 us  [move(): lax.ppermute(pair[0], 'seq', up)]
    all_to_all x3 -> x2, waiting for transfers between devices: 16.9 us -> 15 us  [exchange(): lax.all_to_all(sent.reshape(peers, -1, width), ('tensor', 'pipe'), 0, 0)]
  transfers between devices with their start and end apart: 19 -> 18, of which waited for: 8 -> 6; matrix products, arithmetic and copies ran while one was open for 6% -> 4% of each run, Pallas kernels for 12% -> 18%
where the time goes in v3:
time: 165 us
  starting transfers between devices  54.4 us (33%)
  waiting for transfers between devices  37.5 us (23%)
  Pallas kernels  33.4 us (20%)
  blocking collectives  22 us (13%)
  local copies, waits for them, and re-layouts  7.44 us (5%)
  other arithmetic  5.5 us (3%)
  between operations  2.25 us (1%)
  matrix products  2.22 us (1%)
    pallas_call x4, Pallas kernels, product(): pl.pallas_call(functools.partial(product_kernel, len(pieces), len(extra)...  28.9 us
    ppermute x7, starting transfers between devices, move(): lax.ppermute(pair[1], 'seq', down)  20.8 us
    all_to_all x2, starting transfers between devices, exchange(): lax.all_to_all(sent.reshape(peers, -1, width), ('tensor', 'pipe'), 0, 0)  16.9 us
    all_to_all x2, waiting for transfers between devices, exchange(): lax.all_to_all(sent.reshape(peers, -1, width), ('tensor', 'pipe'), 0, 0)  15 us
    all_to_all x1, blocking collectives, per_device(): lax.all_to_all(partial_cores, ('seq', 'tensor'), 0, 0, tiled=True)  12.6 us
    all_to_all x1, waiting for transfers between devices, per_device(): packed = lax.all_to_all(packed, ('pipe', 'seq'), 0, 0)  9.46 us
    all_to_all x1, blocking collectives, per_device(): lax.all_to_all(jnp.broadcast_to(terms[None], (layers, 2)), 'pipe', 0, 0,...  9.44 us
    ppermute x7, waiting for transfers between devices, move(): lax.ppermute(pair[0], 'seq', up)  8.69 us
  transfers between devices with their start and end apart: 18, of which 6 were waited for; matrix products, arithmetic and copies ran while one was open for 4% of the time, Pallas kernels for 18%

profile of v3, /device:TPU:1, one launch (start us, length us, event | category | flops | bytes accessed | tf_op | source)
XLA Modules:
  0.0 164.7 jit_solution(393560216243979793)
XLA Ops:
  2.2 2.5 %collective-permute-start = (bf16[64,3584]{1,0:T(8,128)(2,1)}, bf16[64,3584]{1,0:T(8,128)(2,1)}, u32[]{:S(2)}, u32[]{:S(2)}) collective-permute-start(bf16[64,3584]{1,0:T(8,128)(2,1)} %get-tuple-element.36), channel_id=1, source_target_pairs={{0,4},{4,8},{8,12},{12,16},{16,20},{20,24},{24,28},{28,0},{1,5},{5... | collective-permute-start | bytes 1376264 | tf_op jit(solution)/shard_map/ppermute | solution.py:202
  4.7 3.9 %collective-permute-start.1 = (bf16[64,3584]{1,0:T(8,128)(2,1)}, bf16[64,3584]{1,0:T(8,128)(2,1)}, u32[]{:S(2)}, u32[]{:S(2)}) collective-permute-start(bf16[64,3584]{1,0:T(8,128)(2,1)} %get-tuple-element.35), channel_id=1, source_target_pairs={{0,28},{4,0},{8,4},{12,8},{16,12},{20,16},{24,20},{28,24},{1,29},{... | collective-permute-start | bytes 1376264 | tf_op jit(solution)/shard_map/ppermute | solution.py:202
  9.7 2.7 %collective-permute-start.5 = (bf16[64,3584]{1,0:T(8,128)(2,1)}, bf16[64,3584]{1,0:T(8,128)(2,1)}, u32[]{:S(2)}, u32[]{:S(2)}) collective-permute-start(bf16[64,3584]{1,0:T(8,128)(2,1)} %get-tuple-element.36), channel_id=1, source_target_pairs={{0,28},{4,0},{8,4},{12,8},{16,12},{20,16},{24,20},{28,24},{1,29},{... | collective-permute-start | bytes 1376264 | tf_op jit(solution)/shard_map/ppermute | solution.py:202
  12.4 5.8 %all-to-all-start = ((f32[8,32,1024]{2,1,0:T(8,128)}), f32[8,32,1024]{2,1,0:T(8,128)S(1)}, u32[]{:S(2)}, u32[]{:S(2)}) async-start(f32[8,32,1024]{2,1,0:T(8,128)} %broadcast_in_dim.88), calls=%async_computation | async-start | bytes 2097152 | tf_op jit(solution)/shard_map/all_to_all | solution.py:230
  21.6 2.7 %collective-permute-start.3 = (bf16[64,3584]{1,0:T(8,128)(2,1)}, bf16[64,3584]{1,0:T(8,128)(2,1)}, u32[]{:S(2)}, u32[]{:S(2)}) collective-permute-start(bf16[64,3584]{1,0:T(8,128)(2,1)} %collective-permute-done.1.refs_2_), channel_id=1, source_target_pairs={{0,28},{4,0},{8,4},{12,8},{16,12},{20,16},{24,20},{28,24},{1,29},{... | collective-permute-start | bytes 1376264 | tf_op jit(solution)/shard_map/ppermute | solution.py:202
  24.3 4.7 %collective-permute-done.4.refs_4_ = bf16[64,3584]{1,0:T(8,128)(2,1)} collective-permute-done((bf16[64,3584]{1,0:T(8,128)(2,1)}, bf16[64,3584]{1,0:T(8,128)(2,1)}, u32[]{:S(2)}, u32[]{:S(2)}) %collective-permute-start.4) | collective-permute-done | bytes 458784 | tf_op jit(solution)/shard_map/ppermute | solution.py:202
  29.0 2.4 %collective-permute-start.8 = (bf16[64,3584]{1,0:T(8,128)(2,1)}, bf16[64,3584]{1,0:T(8,128)(2,1)}, u32[]{:S(2)}, u32[]{:S(2)}) collective-permute-start(bf16[64,3584]{1,0:T(8,128)(2,1)} %collective-permute-done.5.refs_3_), channel_id=1, source_target_pairs={{0,28},{4,0},{8,4},{12,8},{16,12},{20,16},{24,20},{28,24},{1,29},{... | collective-permute-start | bytes 1376264 | tf_op jit(solution)/shard_map/ppermute | solution.py:202
  31.4 9.0 %shard_map.100.refs_8_ = bf16[768,1024]{1,0:T(8,128)(2,1)} custom-call(bf16[128,3584]{1,0:T(8,128)(2,1)} %bitcast.39, bf16[64,3584]{1,0:T(8,128)(2,1)} %collective-permute-done.refs_1_, bf16[64,3584]{1,0:T(8,128)(2,1)} %collective-permute-done.1.refs_2_, bf16[64,3584]{1,0:T(8,128)(2,1)} %collective-permute-done.5.refs_3_, ...), custom_call_target="tpu_custom_call" | custom-call | flops 1150000000 | bytes 65536 | tf_op jit(solution)/shard_map/pallas_call | solution.py:93
  40.5 2.7 %collective-permute-start.7 = (bf16[64,3584]{1,0:T(8,128)(2,1)}, bf16[64,3584]{1,0:T(8,128)(2,1)}, u32[]{:S(2)}, u32[]{:S(2)}) collective-permute-start(bf16[64,3584]{1,0:T(8,128)(2,1)} %collective-permute-done.3.refs_1_), channel_id=1, source_target_pairs={{0,28},{4,0},{8,4},{12,8},{16,12},{20,16},{24,20},{28,24},{1,29},{... | collective-permute-start | bytes 1376264 | tf_op jit(solution)/shard_map/ppermute | solution.py:202
  43.3 4.3 %collective-permute-done.8.refs_2_ = bf16[64,3584]{1,0:T(8,128)(2,1)} collective-permute-done((bf16[64,3584]{1,0:T(8,128)(2,1)}, bf16[64,3584]{1,0:T(8,128)(2,1)}, u32[]{:S(2)}, u32[]{:S(2)}) %collective-permute-start.8) | collective-permute-done | bytes 458784 | tf_op jit(solution)/shard_map/ppermute | solution.py:202
  47.6 3.4 %collective-permute-start.12 = (bf16[64,3584]{1,0:T(8,128)(2,1)}, bf16[64,3584]{1,0:T(8,128)(2,1)}, u32[]{:S(2)}, u32[]{:S(2)}) collective-permute-start(bf16[64,3584]{1,0:T(8,128)(2,1)} %collective-permute-done.8.refs_2_), channel_id=1, source_target_pairs={{0,28},{4,0},{8,4},{12,8},{16,12},{20,16},{24,20},{28,24},{1,29},{... | collective-permute-start | bytes 1376264 | tf_op jit(solution)/shard_map/ppermute | solution.py:202
  52.0 7.5 %shard_map.101 = bf16[768,1024]{1,0:T(8,128)(2,1)} custom-call(bf16[64,3584]{1,0:T(8,128)(2,1)} %collective-permute-done.2.refs_0_, bf16[64,3584]{1,0:T(8,128)(2,1)} %collective-permute-done.3.refs_1_, bf16[64,3584]{1,0:T(8,128)(2,1)} %collective-permute-done.8.refs_2_, bf16[64,3584]{1,0:T(8,128)(2,1)} %collective-permute-done.9.refs_3_, ...), custom_call_target="tpu_custom_call" | custom-call | flops 6899999744 | bytes 65536 | tf_op jit(solution)/shard_map/pallas_call | solution.py:93
  59.4 10.1 %all-to-all-start.1 = ((bf16[32,24,1024]{2,1,0:T(8,128)(2,1)}), bf16[32,24,1024]{2,1,0:T(8,128)(2,1)S(1)}, u32[]{:S(2)}, u32[]{:S(2)}) async-start(bf16[32,24,1024]{2,1,0:T(8,128)(2,1)} %bitcast.44), calls=%async_computation.1 | async-start | bytes 3145728 | tf_op jit(solution)/shard_map/all_to_all | solution.py:221
  69.7 3.0 %collective-permute-start.11 = (bf16[64,3584]{1,0:T(8,128)(2,1)}, bf16[64,3584]{1,0:T(8,128)(2,1)S(1)}, u32[]{:S(2)}, u32[]{:S(2)}) collective-permute-start(bf16[64,3584]{1,0:T(8,128)(2,1)} %collective-permute-done.7.refs_1_), channel_id=1, source_target_pairs={{0,28},{4,0},{8,4},{12,8},{16,12},{20,16},{24,20},{28,24},{1,29},{... | collective-permute-start | bytes 1376264 | tf_op jit(solution)/shard_map/ppermute | solution.py:202
  72.7 6.9 %shard_map.102.refs_4_ = bf16[512,1024]{1,0:T(8,128)(2,1)} custom-call(bf16[64,3584]{1,0:T(8,128)(2,1)} %collective-permute-done.6.refs_0_, bf16[64,3584]{1,0:T(8,128)(2,1)} %collective-permute-done.7.refs_1_, bf16[64,3584]{1,0:T(8,128)(2,1)} %collective-permute-done.12.refs_2_, bf16[64,3584]{1,0:T(8,128)(2,1)} %collective-permute-done.13.refs_3_, ...), custom_call_target="tpu_custom_call" | custom-call | flops 6899999744 | bytes 65536 | tf_op jit(solution)/shard_map/pallas_call | solution.py:93
  79.6 4.0 %collective-permute-done.10.refs_0_ = bf16[64,3584]{1,0:T(8,128)(2,1)S(1)} collective-permute-done((bf16[64,3584]{1,0:T(8,128)(2,1)}, bf16[64,3584]{1,0:T(8,128)(2,1)S(1)}, u32[]{:S(2)}, u32[]{:S(2)}) %collective-permute-start.10) | collective-permute-done | bytes 458784 | tf_op jit(solution)/shard_map/ppermute | solution.py:202
  85.1 5.6 %shard_map.103 = bf16[512,1024]{1,0:T(8,128)(2,1)} custom-call(bf16[64,3584]{1,0:T(8,128)(2,1)} %copy-done.7, bf16[64,3584]{1,0:T(8,128)(2,1)} %copy-done.8, bf16[3584,1024]{1,0:T(8,128)(2,1)} %bitcast.43, bf16[512,128]{1,0:T(8,128)(2,1)S(1)} %fusion.8.refs_3_, bf16[512,1024]{1,0:T(8,128)(2,1)} %shard_map.102.refs_4_), custom_call_target="tpu_custom_call" | custom-call | flops 6899999744 | bytes 65536 | tf_op jit(solution)/shard_map/pallas_call | solution.py:93
  91.7 6.9 %all-to-all-start.2 = ((bf16[32,16,1024]{2,1,0:T(8,128)(2,1)}), bf16[32,16,1024]{2,1,0:T(8,128)(2,1)}, u32[]{:S(2)}, u32[]{:S(2)}) async-start(bf16[32,16,1024]{2,1,0:T(8,128)(2,1)} %bitcast.45), calls=%async_computation.2 | async-start | bytes 2097152 | tf_op jit(solution)/shard_map/all_to_all | solution.py:221
  101.8 14.0 %all-to-all-done.2.got = bf16[32,16,1024]{2,1,0:T(8,128)(2,1)} async-done(((bf16[32,16,1024]{2,1,0:T(8,128)(2,1)}), bf16[32,16,1024]{2,1,0:T(8,128)(2,1)}, u32[]{:S(2)}, u32[]{:S(2)}) %all-to-all-start.2) | async-done | bytes 1048608 | tf_op jit(solution)/shard_map/all_to_all | solution.py:221
  115.8 3.3 %shard_map.105 = f32[64,1,384]{2,1,0:T(1,128)} custom-call(bf16[32,16,1024]{2,1,0:T(8,128)(2,1)} %all-to-all-done.2.got, f32[16,1024]{1,0:T(8,128)S(1)} %slice.75.resid, f32[16,1024]{1,0:T(8,128)S(1)} %slice.77.aim, f32[256,1024]{1,0:T(8,128)S(1)} %bitcast.38, f32[24,256]{1,0:T(8,128)S(1)} %get-tuple-element.59.first, ...), custom_call_target="tpu_custom_call" | custom-call | tf_op jit(solution)/shard_map/pallas_call | solution.py:172
  119.1 8.1 %all-to-all-start.3 = ((f32[64,1,384]{2,1,0:T(1,128)}), f32[64,1,384]{2,1,0:T(1,128)S(1)}, u32[]{:S(2)}, u32[]{:S(2)}) async-start(f32[64,1,384]{2,1,0:T(1,128)} %shard_map.105), calls=%async_computation.3 | async-start | bytes 196608 | tf_op jit(solution)/shard_map/all_to_all | solution.py:319
  127.5 9.5 %all-to-all-done.3 = f32[64,1,384]{2,1,0:T(1,128)S(1)} async-done(((f32[64,1,384]{2,1,0:T(1,128)}), f32[64,1,384]{2,1,0:T(1,128)S(1)}, u32[]{:S(2)}, u32[]{:S(2)}) %all-to-all-start.3) | async-done | bytes 98336 | tf_op jit(solution)/shard_map/all_to_all | solution.py:319
  138.3 12.6 %all_to_all.35 = f32[32,1,1024]{2,1,0:T(1,128)S(1)} all-to-all(f32[32,1,1024]{2,1,0:T(1,128)S(1)} %copy.18), channel_id=1, replica_groups=mesh['pipe'=8,'seq'=8,'tensor'=4] {'seq','tensor'}, dimensions={0} | all-to-all | bytes 262144 | tf_op jit(solution)/shard_map/all_to_all | solution.py:336
  152.9 9.4 %all_to_all.36 = f32[8,1,2]{2,1,0:T(1,128)S(1)} all-to-all(f32[8,1,2]{2,1,0:T(1,128)S(1)} %broadcast_in_dim.96), channel_id=1, replica_groups=mesh['pipe'=8,'seq'=8,'tensor'=4] {'pipe'}, dimensions={0} | all-to-all | bytes 128 | tf_op jit(solution)/shard_map/all_to_all | solution.py:340
  (95 shorter events, 17.6 us)
Async XLA Ops:
  0.0 18.8 %copy-start = (bf16[1,3584,32]{1,2,0:T(8,128)(2,1)S(1)}, bf16[1,3584,32]{1,2,0:T(8,128)(2,1)}, u32[]{:S(2)}) copy-start(bf16[1,3584,32]{1,2,0:T(8,128)(2,1)} %param.16) | copy-start | bytes 688132
  0.0 8.6 %copy-start.3 = (f32[1,1024,32]{1,2,0:T(8,128)S(1)}, f32[1,1024,32]{1,2,0:T(8,128)}, u32[]{:S(2)}) copy-start(f32[1,1024,32]{1,2,0:T(8,128)} %param.15) | copy-start | bytes 393220
  2.2 19.3 %collective-permute-start = (bf16[64,3584]{1,0:T(8,128)(2,1)}, bf16[64,3584]{1,0:T(8,128)(2,1)}, u32[]{:S(2)}, u32[]{:S(2)}) collective-permute-start(bf16[64,3584]{1,0:T(8,128)(2,1)} %get-tuple-element.36), channel_id=1, source_target_pairs={{0,4},{4,8},{8,12},{12,16},{16,20},{20,24},{24,28},{28,0},{1,5},{5... | collective-permute-start | bytes 1376264 | tf_op jit(solution)/shard_map/ppermute | solution.py:202
  4.7 16.9 %collective-permute-start.1 = (bf16[64,3584]{1,0:T(8,128)(2,1)}, bf16[64,3584]{1,0:T(8,128)(2,1)}, u32[]{:S(2)}, u32[]{:S(2)}) collective-permute-start(bf16[64,3584]{1,0:T(8,128)(2,1)} %get-tuple-element.35), channel_id=1, source_target_pairs={{0,28},{4,0},{8,4},{12,8},{16,12},{20,16},{24,20},{28,24},{1,29},{... | collective-permute-start | bytes 1376264 | tf_op jit(solution)/shard_map/ppermute | solution.py:202
  9.7 9.1 %copy-start.2 = (bf16[1,128,3584]{2,1,0:T(8,128)(2,1)S(1)}, bf16[1,128,3584]{2,1,0:T(8,128)(2,1)}, u32[]{:S(2)}) copy-start(bf16[1,128,3584]{2,1,0:T(8,128)(2,1)} %param.10) | copy-start | bytes 2752516
  9.7 19.3 %collective-permute-start.4 = (bf16[64,3584]{1,0:T(8,128)(2,1)}, bf16[64,3584]{1,0:T(8,128)(2,1)}, u32[]{:S(2)}, u32[]{:S(2)}) collective-permute-start(bf16[64,3584]{1,0:T(8,128)(2,1)} %get-tuple-element.35), channel_id=1, source_target_pairs={{0,4},{4,8},{8,12},{12,16},{16,20},{20,24},{24,28},{28,0},{1,5},{5... | collective-permute-start | bytes 1376264 | tf_op jit(solution)/shard_map/ppermute | solution.py:202
  9.7 19.3 %collective-permute-start.5 = (bf16[64,3584]{1,0:T(8,128)(2,1)}, bf16[64,3584]{1,0:T(8,128)(2,1)}, u32[]{:S(2)}, u32[]{:S(2)}) collective-permute-start(bf16[64,3584]{1,0:T(8,128)(2,1)} %get-tuple-element.36), channel_id=1, source_target_pairs={{0,28},{4,0},{8,4},{12,8},{16,12},{20,16},{24,20},{28,24},{1,29},{... | collective-permute-start | bytes 1376264 | tf_op jit(solution)/shard_map/ppermute | solution.py:202
  12.4 28.0 %all-to-all-start = ((f32[8,32,1024]{2,1,0:T(8,128)}), f32[8,32,1024]{2,1,0:T(8,128)S(1)}, u32[]{:S(2)}, u32[]{:S(2)}) async-start(f32[8,32,1024]{2,1,0:T(8,128)} %broadcast_in_dim.88), calls=%async_computation | async-start | bytes 2097152 | tf_op jit(solution)/shard_map/all_to_all | solution.py:230
  21.5 18.9 %collective-permute-start.2 = (bf16[64,3584]{1,0:T(8,128)(2,1)}, bf16[64,3584]{1,0:T(8,128)(2,1)}, u32[]{:S(2)}, u32[]{:S(2)}) collective-permute-start(bf16[64,3584]{1,0:T(8,128)(2,1)} %collective-permute-done.refs_1_), channel_id=1, source_target_pairs={{0,4},{4,8},{8,12},{12,16},{16,20},{20,24},{24,28},{28,0},{1,5},{5... | collective-permute-start | bytes 1376264 | tf_op jit(solution)/shard_map/ppermute | solution.py:202
  21.6 18.8 %collective-permute-start.3 = (bf16[64,3584]{1,0:T(8,128)(2,1)}, bf16[64,3584]{1,0:T(8,128)(2,1)}, u32[]{:S(2)}, u32[]{:S(2)}) collective-permute-start(bf16[64,3584]{1,0:T(8,128)(2,1)} %collective-permute-done.1.refs_2_), channel_id=1, source_target_pairs={{0,28},{4,0},{8,4},{12,8},{16,12},{20,16},{24,20},{28,24},{1,29},{... | collective-permute-start | bytes 1376264 | tf_op jit(solution)/shard_map/ppermute | solution.py:202
  29.0 18.6 %collective-permute-start.8 = (bf16[64,3584]{1,0:T(8,128)(2,1)}, bf16[64,3584]{1,0:T(8,128)(2,1)}, u32[]{:S(2)}, u32[]{:S(2)}) collective-permute-start(bf16[64,3584]{1,0:T(8,128)(2,1)} %collective-permute-done.5.refs_3_), channel_id=1, source_target_pairs={{0,28},{4,0},{8,4},{12,8},{16,12},{20,16},{24,20},{28,24},{1,29},{... | collective-permute-start | bytes 1376264 | tf_op jit(solution)/shard_map/ppermute | solution.py:202
  31.4 19.7 %collective-permute-start.9 = (bf16[64,3584]{1,0:T(8,128)(2,1)}, bf16[64,3584]{1,0:T(8,128)(2,1)}, u32[]{:S(2)}, u32[]{:S(2)}) collective-permute-start(bf16[64,3584]{1,0:T(8,128)(2,1)} %collective-permute-done.4.refs_4_), channel_id=1, source_target_pairs={{0,4},{4,8},{8,12},{12,16},{16,20},{20,24},{24,28},{28,0},{1,5},{5... | collective-permute-start | bytes 1376264 | tf_op jit(solution)/shard_map/ppermute | solution.py:202
  40.4 29.1 %collective-permute-start.6 = (bf16[64,3584]{1,0:T(8,128)(2,1)}, bf16[64,3584]{1,0:T(8,128)(2,1)}, u32[]{:S(2)}, u32[]{:S(2)}) collective-permute-start(bf16[64,3584]{1,0:T(8,128)(2,1)} %collective-permute-done.2.refs_0_), channel_id=1, source_target_pairs={{0,4},{4,8},{8,12},{12,16},{16,20},{20,24},{24,28},{28,0},{1,5},{5... | collective-permute-start | bytes 1376264 | tf_op jit(solution)/shard_map/ppermute | solution.py:202
  40.5 29.0 %collective-permute-start.7 = (bf16[64,3584]{1,0:T(8,128)(2,1)}, bf16[64,3584]{1,0:T(8,128)(2,1)}, u32[]{:S(2)}, u32[]{:S(2)}) collective-permute-start(bf16[64,3584]{1,0:T(8,128)(2,1)} %collective-permute-done.3.refs_1_), channel_id=1, source_target_pairs={{0,28},{4,0},{8,4},{12,8},{16,12},{20,16},{24,20},{28,24},{1,29},{... | collective-permute-start | bytes 1376264 | tf_op jit(solution)/shard_map/ppermute | solution.py:202
  47.6 25.1 %collective-permute-start.12 = (bf16[64,3584]{1,0:T(8,128)(2,1)}, bf16[64,3584]{1,0:T(8,128)(2,1)}, u32[]{:S(2)}, u32[]{:S(2)}) collective-permute-start(bf16[64,3584]{1,0:T(8,128)(2,1)} %collective-permute-done.8.refs_2_), channel_id=1, source_target_pairs={{0,28},{4,0},{8,4},{12,8},{16,12},{20,16},{24,20},{28,24},{1,29},{... | collective-permute-start | bytes 1376264 | tf_op jit(solution)/shard_map/ppermute | solution.py:202
  51.0 21.7 %collective-permute-start.13 = (bf16[64,3584]{1,0:T(8,128)(2,1)}, bf16[64,3584]{1,0:T(8,128)(2,1)}, u32[]{:S(2)}, u32[]{:S(2)}) collective-permute-start(bf16[64,3584]{1,0:T(8,128)(2,1)} %collective-permute-done.9.refs_3_), channel_id=1, source_target_pairs={{0,4},{4,8},{8,12},{12,16},{16,20},{20,24},{24,28},{28,0},{1,5},{5... | collective-permute-start | bytes 1376264 | tf_op jit(solution)/shard_map/ppermute | solution.py:202
  59.4 32.3 %all-to-all-start.1 = ((bf16[32,24,1024]{2,1,0:T(8,128)(2,1)}), bf16[32,24,1024]{2,1,0:T(8,128)(2,1)S(1)}, u32[]{:S(2)}, u32[]{:S(2)}) async-start(bf16[32,24,1024]{2,1,0:T(8,128)(2,1)} %bitcast.44), calls=%async_computation.1 | async-start | bytes 3145728 | tf_op jit(solution)/shard_map/all_to_all | solution.py:221
  69.6 14.0 %collective-permute-start.10 = (bf16[64,3584]{1,0:T(8,128)(2,1)}, bf16[64,3584]{1,0:T(8,128)(2,1)S(1)}, u32[]{:S(2)}, u32[]{:S(2)}) collective-permute-start(bf16[64,3584]{1,0:T(8,128)(2,1)} %collective-permute-done.6.refs_0_), channel_id=1, source_target_pairs={{0,4},{4,8},{8,12},{12,16},{16,20},{20,24},{24,28},{28,0},{1,5},{5... | collective-permute-start | bytes 1376264 | tf_op jit(solution)/shard_map/ppermute | solution.py:202
  69.7 13.9 %collective-permute-start.11 = (bf16[64,3584]{1,0:T(8,128)(2,1)}, bf16[64,3584]{1,0:T(8,128)(2,1)S(1)}, u32[]{:S(2)}, u32[]{:S(2)}) collective-permute-start(bf16[64,3584]{1,0:T(8,128)(2,1)} %collective-permute-done.7.refs_1_), channel_id=1, source_target_pairs={{0,28},{4,0},{8,4},{12,8},{16,12},{20,16},{24,20},{28,24},{1,29},{... | collective-permute-start | bytes 1376264 | tf_op jit(solution)/shard_map/ppermute | solution.py:202
  90.7 7.9 %copy-start.9 = (s32[32]{0:T(128)S(1)}, s32[32]{0:T(128)}, u32[]{:S(2)}) copy-start(s32[32]{0:T(128)} %param.19) | copy-start | bytes 388
  91.7 24.1 %all-to-all-start.2 = ((bf16[32,16,1024]{2,1,0:T(8,128)(2,1)}), bf16[32,16,1024]{2,1,0:T(8,128)(2,1)}, u32[]{:S(2)}, u32[]{:S(2)}) async-start(bf16[32,16,1024]{2,1,0:T(8,128)(2,1)} %bitcast.45), calls=%async_computation.2 | async-start | bytes 2097152 | tf_op jit(solution)/shard_map/all_to_all | solution.py:221
  119.1 31.9 %copy-start.5 = (f32[1,1024]{1,0:T(1,128)S(1)}, f32[1,1024]{1,0:T(1,128)}, u32[]{:S(2)}) copy-start(f32[1,1024]{1,0:T(1,128)} %param.17) | copy-start | bytes 12292
  119.1 31.9 %copy-start.6 = (f32[1,1024]{1,0:T(1,128)S(1)}, f32[1,1024]{1,0:T(1,128)}, u32[]{:S(2)}) copy-start(f32[1,1024]{1,0:T(1,128)} %param.18) | copy-start | bytes 12292
  119.1 17.8 %all-to-all-start.3 = ((f32[64,1,384]{2,1,0:T(1,128)}), f32[64,1,384]{2,1,0:T(1,128)S(1)}, u32[]{:S(2)}, u32[]{:S(2)}) async-start(f32[64,1,384]{2,1,0:T(1,128)} %shard_map.105), calls=%async_computation.3 | async-start | bytes 196608 | tf_op jit(solution)/shard_map/all_to_all | solution.py:319
  (4 other events, 9.9 us)

commit v4 on v3

--- a/solution.py
+++ b/solution.py
@@ -87,13 +87,12 @@
     anywhere, held = pl.BlockSpec(memory_space=pltpu.HBM), pl.BlockSpec(memory_space=pltpu.VMEM)
     far = pltpu.with_memory_space_constraint
     weight = pltpu.with_memory_space_constraint(weight, pltpu.HBM)
-    pieces = [far(p, pltpu.HBM) for p in pieces]
     bases = [far(base, pltpu.HBM)] if based else []
     small = [order, *extra]
     return pl.pallas_call(
         functools.partial(product_kernel, len(pieces), len(extra) // 2, based),
         out_shape=pltpu.HBM((height, width), BF16),
-        in_specs=[anywhere] * len(pieces) + [pl.BlockSpec(memory_space=pltpu.HBM)] + [held] * len(small) + [anywhere] * len(bases),
+        in_specs=[pl.BlockSpec(memory_space=pl.ANY)] * len(pieces) + [pl.BlockSpec(memory_space=pltpu.HBM)] + [held] * len(small) + [anywhere] * len(bases),
         out_specs=anywhere,
         scratch_shapes=[
             pltpu.VMEM((total, depth), BF16),
@@ -252,32 +251,33 @@
         ),
         128,
     )
-    orders = units(near, 0, 3), units(near, 3, 2), units(far, 0, 2), units(far, 2, 1)
+    orders = units(near, 0, 3), units(near, 3, 1), units(far, 0, 3), units(far, 3, 1)
     orders, aside_order, right_order, a1, aside = tie((orders, aside_order, right_order, a1, aside))
 
     a2 = move(a1)
     b1, right_rows = tie((b1, right_rows))
     b2 = move(b1)
     sent = product(1,
-        [own, a1[0], a1[1], b1[1], b1[0]], weight, orders[0], (aside_order, aside)
+        [own, a1[0], a1[1], b1[1], b1[0]], weight, orders[0], (aside_order, aside, right_order, right_rows)
     )
     a2, sent, left_all = tie((a2, sent, left_all))
     a3 = move(a2)
+    sent = product(6, [a2[0], a2[1]], weight, orders[1], base=sent)
+    b2, sent = tie((b2, sent))
     b3 = move(b2)
-    sent = product(6,
-        [a2[0], a2[1], b2[1], b2[0]], weight, orders[1], (right_order, right_rows), base=sent
-    )
     got_near = exchange(sent)
     a3, sent = tie((a3, sent))
     a4 = move(a3)
-    sent = product(6, [a3[0], a3[1], b3[1], b3[0]], weight, orders[2])
+    sent = product(
+        6, [b2[1], b2[0], a3[0], a3[1], b3[1], b3[0]], weight, orders[2]
+    )
     a4, sent = tie((a4, sent))
     sent = product(6, list(a4), weight, orders[3], base=sent)
     sent, got_near = tie((sent, got_near))
     got_far = exchange(sent)
 
     turned = jnp.where(tensor < tensors // 2, 1, -1)
-    slots = [0, -1, 1, -2, 2, None, -3, 3, seqs // 2, None]
+    slots = [0, -1, 1, -2, None, None, 2, -3, 3, seqs // 2]
     slot = column(len(slots) * share)
     offset = jnp.zeros_like(slot)
     filled = jnp.ones_like(slot)
@@ -335,10 +335,9 @@
     partial_cores = jnp.dot(member, outer, precision=lax.Precision.HIGHEST)
     cores = jnp.sum(lax.all_to_all(partial_cores, ("seq", "tensor"), 0, 0, tiled=True), axis=0)
     scaled = cores / eigen[0]
-    terms = jnp.stack([jnp.sum(query_core[0] * scaled), jnp.sum(cores * scaled)])
-    terms = jnp.sum(
-        lax.all_to_all(jnp.broadcast_to(terms[None], (layers, 2)), "pipe", 0, 0, tiled=True), axis=0
-    )
+    score, own_term = jnp.sum(query_core[0] * scaled), jnp.sum(cores * scaled)
+    terms = jnp.where(lax.broadcasted_iota(jnp.int32, (layers, 2), 1) == 0, score, own_term)
+    terms = jnp.sum(lax.all_to_all(terms, "pipe", 0, 0, tiled=True), axis=0)
     return (terms[0] / jnp.sqrt(terms[1] + 1e-06)).reshape(1)
 
 

time: 165 us -> 158 us (0.958)
  waiting for transfers between devices: 37.5 us -> 32.9 us
  starting transfers between devices: 54.4 us -> 52.4 us
    ppermute x7, starting transfers between devices: 20.8 us -> 17.9 us  [move(): lax.ppermute(pair[1], 'seq', down)]
    ppermute x7, waiting for transfers between devices: 8.69 us -> 5.75 us  [move(): lax.ppermute(pair[0], 'seq', up)]
    ppermute x7, waiting for transfers between devices: 4.34 us -> 1.45 us  [move(): lax.ppermute(pair[1], 'seq', down)]
  transfers between devices with their start and end apart: 18 -> 18, of which waited for: 6 -> 7; matrix products, arithmetic and copies ran while one was open for 4% -> 5% of each run, Pallas kernels for 18% -> 19%
where the time goes in v4:
time: 158 us; the launch traced here: 157 us
  starting transfers between devices  52.4 us (33%)
  waiting for transfers between devices  32.9 us (21%)
  Pallas kernels  32.9 us (21%)
  blocking collectives  22.1 us (14%)
  other arithmetic  6.81 us (4%)
  local copies, waits for them, and re-layouts  5.97 us (4%)
  between operations  2.25 us (1%)
  matrix products  2.22 us (1%)
    pallas_call x4, Pallas kernels, product(): pl.pallas_call(functools.partial(product_kernel, len(pieces), len(extra)...  28.5 us
    ppermute x7, starting transfers between devices, move(): lax.ppermute(pair[1], 'seq', down)  17.9 us
    all_to_all x2, starting transfers between devices, exchange(): lax.all_to_all(sent.reshape(peers, -1, width), ('tensor', 'pipe'), 0, 0)  17.4 us
    all_to_all x2, waiting for transfers between devices, exchange(): lax.all_to_all(sent.reshape(peers, -1, width), ('tensor', 'pipe'), 0, 0)  16.2 us
    all_to_all x1, blocking collectives, per_device(): lax.all_to_all(partial_cores, ('seq', 'tensor'), 0, 0, tiled=True)  12.7 us
    all_to_all x1, waiting for transfers between devices, per_device(): packed = lax.all_to_all(packed, ('pipe', 'seq'), 0, 0)  9.46 us
    all_to_all x1, blocking collectives, per_device(): terms = jnp.sum(lax.all_to_all(terms, 'pipe', 0, 0, tiled=True), axis=0)  9.4 us
    all_to_all x1, starting transfers between devices, per_device(): packed = lax.all_to_all(packed, ('pipe', 'seq'), 0, 0)  7.73 us
  transfers between devices with their start and end apart: 18, of which 7 were waited for; matrix products, arithmetic and copies ran while one was open for 5% of the time, Pallas kernels for 19%

profile of v4, /device:TPU:1, one launch (start us, length us, event | category | flops | bytes accessed | tf_op | source)
XLA Modules:
  0.0 157.5 jit_solution(14903014518889569170)
XLA Ops:
  0.0 2.2 %slice_bitcast_fusion = (bf16[64,3584]{1,0:T(8,128)(2,1)}, bf16[64,3584]{1,0:T(8,128)(2,1)}) fusion(bf16[1,128,3584]{2,1,0:T(8,128)(2,1)} %param.10), kind=kLoop, calls=%fused_computation.9 | loop fusion | bytes 1835008 | tf_op jit(solution)/shard_map/slice | solution.py:222
  2.2 2.5 %collective-permute-start = (bf16[64,3584]{1,0:T(8,128)(2,1)}, bf16[64,3584]{1,0:T(8,128)(2,1)}, u32[]{:S(2)}, u32[]{:S(2)}) collective-permute-start(bf16[64,3584]{1,0:T(8,128)(2,1)} %get-tuple-element.39), channel_id=1, source_target_pairs={{0,4},{4,8},{8,12},{12,16},{16,20},{20,24},{24,28},{28,0},{1,5},{5... | collective-permute-start | bytes 1376264 | tf_op jit(solution)/shard_map/ppermute | solution.py:201
  4.7 3.9 %collective-permute-start.1 = (bf16[64,3584]{1,0:T(8,128)(2,1)}, bf16[64,3584]{1,0:T(8,128)(2,1)}, u32[]{:S(2)}, u32[]{:S(2)}) collective-permute-start(bf16[64,3584]{1,0:T(8,128)(2,1)} %get-tuple-element.38), channel_id=1, source_target_pairs={{0,28},{4,0},{8,4},{12,8},{16,12},{20,16},{24,20},{28,24},{1,29},{... | collective-permute-start | bytes 1376264 | tf_op jit(solution)/shard_map/ppermute | solution.py:201
  9.8 2.7 %collective-permute-start.5 = (bf16[64,3584]{1,0:T(8,128)(2,1)}, bf16[64,3584]{1,0:T(8,128)(2,1)}, u32[]{:S(2)}, u32[]{:S(2)}) collective-permute-start(bf16[64,3584]{1,0:T(8,128)(2,1)} %get-tuple-element.39), channel_id=1, source_target_pairs={{0,28},{4,0},{8,4},{12,8},{16,12},{20,16},{24,20},{28,24},{1,29},{... | collective-permute-start | bytes 1376264 | tf_op jit(solution)/shard_map/ppermute | solution.py:201
  12.4 5.8 %all-to-all-start = ((f32[8,32,1024]{2,1,0:T(8,128)}), f32[8,32,1024]{2,1,0:T(8,128)S(1)}, u32[]{:S(2)}, u32[]{:S(2)}) async-start(f32[8,32,1024]{2,1,0:T(8,128)} %broadcast_in_dim.90), calls=%async_computation | async-start | bytes 2097152 | tf_op jit(solution)/shard_map/all_to_all | solution.py:229
  22.5 2.7 %collective-permute-start.3 = (bf16[64,3584]{1,0:T(8,128)(2,1)}, bf16[64,3584]{1,0:T(8,128)(2,1)}, u32[]{:S(2)}, u32[]{:S(2)}) collective-permute-start(bf16[64,3584]{1,0:T(8,128)(2,1)} %collective-permute-done.1.refs_2_), channel_id=1, source_target_pairs={{0,28},{4,0},{8,4},{12,8},{16,12},{20,16},{24,20},{28,24},{1,29},{... | collective-permute-start | bytes 1376264 | tf_op jit(solution)/shard_map/ppermute | solution.py:201
  25.6 3.4 %collective-permute-done.4.refs_4_ = bf16[64,3584]{1,0:T(8,128)(2,1)} collective-permute-done((bf16[64,3584]{1,0:T(8,128)(2,1)}, bf16[64,3584]{1,0:T(8,128)(2,1)}, u32[]{:S(2)}, u32[]{:S(2)}) %collective-permute-start.4) | collective-permute-done | bytes 458784 | tf_op jit(solution)/shard_map/ppermute | solution.py:201
  29.0 2.7 %collective-permute-start.9 = (bf16[64,3584]{1,0:T(8,128)(2,1)}, bf16[64,3584]{1,0:T(8,128)(2,1)}, u32[]{:S(2)}, u32[]{:S(2)}) collective-permute-start(bf16[64,3584]{1,0:T(8,128)(2,1)} %collective-permute-done.5.refs_3_), channel_id=1, source_target_pairs={{0,28},{4,0},{8,4},{12,8},{16,12},{20,16},{24,20},{28,24},{1,29},{... | collective-permute-start | bytes 1376264 | tf_op jit(solution)/shard_map/ppermute | solution.py:201
  31.7 9.2 %shard_map.100.refs_4_ = bf16[768,1024]{1,0:T(8,128)(2,1)} custom-call(bf16[128,3584]{1,0:T(8,128)(2,1)S(1)} %bitcast.37, bf16[64,3584]{1,0:T(8,128)(2,1)} %collective-permute-done.refs_1_, bf16[64,3584]{1,0:T(8,128)(2,1)} %collective-permute-done.1.refs_2_, bf16[64,3584]{1,0:T(8,128)(2,1)} %collective-permute-done.5.refs_3_, ...), custom_call_target="tpu_custom_call" | custom-call | flops 1150000000 | bytes 65536 | tf_op jit(solution)/shard_map/pallas_call | solution.py:92
  41.1 2.7 %collective-permute-start.7 = (bf16[64,3584]{1,0:T(8,128)(2,1)}, bf16[64,3584]{1,0:T(8,128)(2,1)}, u32[]{:S(2)}, u32[]{:S(2)}) collective-permute-start(bf16[64,3584]{1,0:T(8,128)(2,1)} %collective-permute-done.3.refs_1_), channel_id=1, source_target_pairs={{0,28},{4,0},{8,4},{12,8},{16,12},{20,16},{24,20},{28,24},{1,29},{... | collective-permute-start | bytes 1376264 | tf_op jit(solution)/shard_map/ppermute | solution.py:201
  44.6 5.8 %shard_map.101 = bf16[768,1024]{1,0:T(8,128)(2,1)} custom-call(bf16[64,3584]{1,0:T(8,128)(2,1)} %collective-permute-done.2.refs_0_, bf16[64,3584]{1,0:T(8,128)(2,1)} %collective-permute-done.3.refs_1_, bf16[3584,1024]{1,0:T(8,128)(2,1)} %bitcast.39, bf16[768,128]{1,0:T(8,128)(2,1)S(1)} %copy-done.3, bf16[768,1024]{1,0:T(8,128)(2,1)} %shard_map.100.refs_4_), custom_call_target="tpu_custom_call" | custom-call | flops 6899999744 | bytes 65536 | tf_op jit(solution)/shard_map/pallas_call | solution.py:92
  52.0 11.0 %all-to-all-start.1 = ((bf16[32,24,1024]{2,1,0:T(8,128)(2,1)}), bf16[32,24,1024]{2,1,0:T(8,128)(2,1)S(1)}, u32[]{:S(2)}, u32[]{:S(2)}) async-start(bf16[32,24,1024]{2,1,0:T(8,128)(2,1)} %bitcast.42), calls=%async_computation.1 | async-start | bytes 3145728 | tf_op jit(solution)/shard_map/all_to_all | solution.py:220
  63.2 2.7 %collective-permute-start.11 = (bf16[64,3584]{1,0:T(8,128)(2,1)}, bf16[64,3584]{1,0:T(8,128)(2,1)S(1)}, u32[]{:S(2)}, u32[]{:S(2)}) collective-permute-start(bf16[64,3584]{1,0:T(8,128)(2,1)} %collective-permute-done.7.refs_3_), channel_id=1, source_target_pairs={{0,28},{4,0},{8,4},{12,8},{16,12},{20,16},{24,20},{28,24},{1,29},{... | collective-permute-start | bytes 1376264 | tf_op jit(solution)/shard_map/ppermute | solution.py:201
  65.9 1.4 collective-permute-done.12.refs_4_
  68.4 8.4 %shard_map.102.refs_4_ = bf16[512,1024]{1,0:T(8,128)(2,1)} custom-call(bf16[64,3584]{1,0:T(8,128)(2,1)} %collective-permute-done.9.refs_0_, bf16[64,3584]{1,0:T(8,128)(2,1)} %collective-permute-done.8.refs_1_, bf16[64,3584]{1,0:T(8,128)(2,1)} %collective-permute-done.6.refs_2_, bf16[64,3584]{1,0:T(8,128)(2,1)} %collective-permute-done.7.refs_3_, ...), custom_call_target="tpu_custom_call" | custom-call | flops 6899999744 | bytes 65536 | tf_op jit(solution)/shard_map/pallas_call | solution.py:92
  78.1 5.1 %shard_map.103 = bf16[512,1024]{1,0:T(8,128)(2,1)} custom-call(bf16[64,3584]{1,0:T(8,128)(2,1)S(1)} %collective-permute-done.10.refs_0_, bf16[64,3584]{1,0:T(8,128)(2,1)S(1)} %collective-permute-done.11.refs_1_, bf16[3584,1024]{1,0:T(8,128)(2,1)} %bitcast.41, bf16[512,128]{1,0:T(8,128)(2,1)S(1)} %copy-done.4, bf16[512,1024]{1,0:T(8,128)(2,1)} %shard_map.102.refs_4_), custom_call_target="tpu_custom_call" | custom-call | flops 6899999744 | bytes 65536 | tf_op jit(solution)/shard_map/pallas_call | solution.py:92
  83.2 2.1 %all-to-all-done.1.got = bf16[32,24,1024]{2,1,0:T(8,128)(2,1)S(1)} async-done(((bf16[32,24,1024]{2,1,0:T(8,128)(2,1)}), bf16[32,24,1024]{2,1,0:T(8,128)(2,1)S(1)}, u32[]{:S(2)}, u32[]{:S(2)}) %all-to-all-start.1) | async-done | bytes 1572896 | tf_op jit(solution)/shard_map/all_to_all | solution.py:220
  85.2 6.4 %all-to-all-start.2 = ((bf16[32,16,1024]{2,1,0:T(8,128)(2,1)}), bf16[32,16,1024]{2,1,0:T(8,128)(2,1)}, u32[]{:S(2)}, u32[]{:S(2)}) async-start(bf16[32,16,1024]{2,1,0:T(8,128)(2,1)} %bitcast.43), calls=%async_computation.2 | async-start | bytes 2097152 | tf_op jit(solution)/shard_map/all_to_all | solution.py:220
  94.8 14.2 %all-to-all-done.2.got = bf16[32,16,1024]{2,1,0:T(8,128)(2,1)} async-done(((bf16[32,16,1024]{2,1,0:T(8,128)(2,1)}), bf16[32,16,1024]{2,1,0:T(8,128)(2,1)}, u32[]{:S(2)}, u32[]{:S(2)}) %all-to-all-start.2) | async-done | bytes 1048608 | tf_op jit(solution)/shard_map/all_to_all | solution.py:220
  108.9 3.3 %shard_map.105 = f32[64,1,384]{2,1,0:T(1,128)} custom-call(bf16[32,16,1024]{2,1,0:T(8,128)(2,1)} %all-to-all-done.2.got, f32[16,1024]{1,0:T(8,128)S(1)} %slice.75.resid, f32[16,1024]{1,0:T(8,128)S(1)} %slice.77.aim, f32[256,1024]{1,0:T(8,128)S(1)} %bitcast.36, f32[24,256]{1,0:T(8,128)S(1)} %get-tuple-element.65.first, ...), custom_call_target="tpu_custom_call" | custom-call | tf_op jit(solution)/shard_map/pallas_call | solution.py:171
  112.2 7.7 %all-to-all-start.3 = ((f32[64,1,384]{2,1,0:T(1,128)}), f32[64,1,384]{2,1,0:T(1,128)S(1)}, u32[]{:S(2)}, u32[]{:S(2)}) async-start(f32[64,1,384]{2,1,0:T(1,128)} %shard_map.105), calls=%async_computation.3 | async-start | bytes 196608 | tf_op jit(solution)/shard_map/all_to_all | solution.py:319
  120.3 9.5 %all-to-all-done.3 = f32[64,1,384]{2,1,0:T(1,128)S(1)} async-done(((f32[64,1,384]{2,1,0:T(1,128)}), f32[64,1,384]{2,1,0:T(1,128)S(1)}, u32[]{:S(2)}, u32[]{:S(2)}) %all-to-all-start.3) | async-done | bytes 98336 | tf_op jit(solution)/shard_map/all_to_all | solution.py:319
  131.1 12.7 %all_to_all.35 = f32[32,1,1024]{2,1,0:T(1,128)S(1)} all-to-all(f32[32,1,1024]{2,1,0:T(1,128)S(1)} %copy.18), channel_id=1, replica_groups=mesh['pipe'=8,'seq'=8,'tensor'=4] {'seq','tensor'}, dimensions={0} | all-to-all | bytes 262144 | tf_op jit(solution)/shard_map/all_to_all | solution.py:336
  145.7 9.4 %all_to_all.36 = f32[8,1,2]{2,1,0:T(1,128)S(1)} all-to-all(f32[8,1,2]{2,1,0:T(1,128)S(1)} %iota.105), channel_id=1, replica_groups=mesh['pipe'=8,'seq'=8,'tensor'=4] {'pipe'}, dimensions={0} | all-to-all | bytes 128 | tf_op jit(solution)/shard_map/all_to_all | solution.py:340
  (95 shorter events, 18.0 us)
Async XLA Ops:
  0.0 25.1 %copy-start = (bf16[1,3584,32]{1,2,0:T(8,128)(2,1)S(1)}, bf16[1,3584,32]{1,2,0:T(8,128)(2,1)}, u32[]{:S(2)}) copy-start(bf16[1,3584,32]{1,2,0:T(8,128)(2,1)} %param.16) | copy-start | bytes 688132
  0.0 8.7 %copy-start.5 = (f32[1,1024,32]{1,2,0:T(8,128)S(1)}, f32[1,1024,32]{1,2,0:T(8,128)}, u32[]{:S(2)}) copy-start(f32[1,1024,32]{1,2,0:T(8,128)} %param.15) | copy-start | bytes 393220
  2.2 20.2 %collective-permute-start = (bf16[64,3584]{1,0:T(8,128)(2,1)}, bf16[64,3584]{1,0:T(8,128)(2,1)}, u32[]{:S(2)}, u32[]{:S(2)}) collective-permute-start(bf16[64,3584]{1,0:T(8,128)(2,1)} %get-tuple-element.39), channel_id=1, source_target_pairs={{0,4},{4,8},{8,12},{12,16},{16,20},{20,24},{24,28},{28,0},{1,5},{5... | collective-permute-start | bytes 1376264 | tf_op jit(solution)/shard_map/ppermute | solution.py:201
  4.7 17.7 %collective-permute-start.1 = (bf16[64,3584]{1,0:T(8,128)(2,1)}, bf16[64,3584]{1,0:T(8,128)(2,1)}, u32[]{:S(2)}, u32[]{:S(2)}) collective-permute-start(bf16[64,3584]{1,0:T(8,128)(2,1)} %get-tuple-element.38), channel_id=1, source_target_pairs={{0,28},{4,0},{8,4},{12,8},{16,12},{20,16},{24,20},{28,24},{1,29},{... | collective-permute-start | bytes 1376264 | tf_op jit(solution)/shard_map/ppermute | solution.py:201
  9.8 19.3 %collective-permute-start.4 = (bf16[64,3584]{1,0:T(8,128)(2,1)}, bf16[64,3584]{1,0:T(8,128)(2,1)}, u32[]{:S(2)}, u32[]{:S(2)}) collective-permute-start(bf16[64,3584]{1,0:T(8,128)(2,1)} %get-tuple-element.38), channel_id=1, source_target_pairs={{0,4},{4,8},{8,12},{12,16},{16,20},{20,24},{24,28},{28,0},{1,5},{5... | collective-permute-start | bytes 1376264 | tf_op jit(solution)/shard_map/ppermute | solution.py:201
  9.8 19.3 %collective-permute-start.5 = (bf16[64,3584]{1,0:T(8,128)(2,1)}, bf16[64,3584]{1,0:T(8,128)(2,1)}, u32[]{:S(2)}, u32[]{:S(2)}) collective-permute-start(bf16[64,3584]{1,0:T(8,128)(2,1)} %get-tuple-element.39), channel_id=1, source_target_pairs={{0,28},{4,0},{8,4},{12,8},{16,12},{20,16},{24,20},{28,24},{1,29},{... | collective-permute-start | bytes 1376264 | tf_op jit(solution)/shard_map/ppermute | solution.py:201
  12.4 28.5 %all-to-all-start = ((f32[8,32,1024]{2,1,0:T(8,128)}), f32[8,32,1024]{2,1,0:T(8,128)S(1)}, u32[]{:S(2)}, u32[]{:S(2)}) async-start(f32[8,32,1024]{2,1,0:T(8,128)} %broadcast_in_dim.90), calls=%async_computation | async-start | bytes 2097152 | tf_op jit(solution)/shard_map/all_to_all | solution.py:229
  22.4 18.5 %collective-permute-start.2 = (bf16[64,3584]{1,0:T(8,128)(2,1)}, bf16[64,3584]{1,0:T(8,128)(2,1)}, u32[]{:S(2)}, u32[]{:S(2)}) collective-permute-start(bf16[64,3584]{1,0:T(8,128)(2,1)} %collective-permute-done.refs_1_), channel_id=1, source_target_pairs={{0,4},{4,8},{8,12},{12,16},{16,20},{20,24},{24,28},{28,0},{1,5},{5... | collective-permute-start | bytes 1376264 | tf_op jit(solution)/shard_map/ppermute | solution.py:201
  22.5 18.5 %collective-permute-start.3 = (bf16[64,3584]{1,0:T(8,128)(2,1)}, bf16[64,3584]{1,0:T(8,128)(2,1)}, u32[]{:S(2)}, u32[]{:S(2)}) collective-permute-start(bf16[64,3584]{1,0:T(8,128)(2,1)} %collective-permute-done.1.refs_2_), channel_id=1, source_target_pairs={{0,28},{4,0},{8,4},{12,8},{16,12},{20,16},{24,20},{28,24},{1,29},{... | collective-permute-start | bytes 1376264 | tf_op jit(solution)/shard_map/ppermute | solution.py:201
  29.0 21.4 %collective-permute-start.8 = (bf16[64,3584]{1,0:T(8,128)(2,1)}, bf16[64,3584]{1,0:T(8,128)(2,1)}, u32[]{:S(2)}, u32[]{:S(2)}) collective-permute-start(bf16[64,3584]{1,0:T(8,128)(2,1)} %collective-permute-done.4.refs_4_), channel_id=1, source_target_pairs={{0,4},{4,8},{8,12},{12,16},{16,20},{20,24},{24,28},{28,0},{1,5},{5... | collective-permute-start | bytes 1376264 | tf_op jit(solution)/shard_map/ppermute | solution.py:201
  29.0 21.4 %collective-permute-start.9 = (bf16[64,3584]{1,0:T(8,128)(2,1)}, bf16[64,3584]{1,0:T(8,128)(2,1)}, u32[]{:S(2)}, u32[]{:S(2)}) collective-permute-start(bf16[64,3584]{1,0:T(8,128)(2,1)} %collective-permute-done.5.refs_3_), channel_id=1, source_target_pairs={{0,28},{4,0},{8,4},{12,8},{16,12},{20,16},{24,20},{28,24},{1,29},{... | collective-permute-start | bytes 1376264 | tf_op jit(solution)/shard_map/ppermute | solution.py:201
  41.0 22.1 %collective-permute-start.6 = (bf16[64,3584]{1,0:T(8,128)(2,1)}, bf16[64,3584]{1,0:T(8,128)(2,1)}, u32[]{:S(2)}, u32[]{:S(2)}) collective-permute-start(bf16[64,3584]{1,0:T(8,128)(2,1)} %collective-permute-done.2.refs_0_), channel_id=1, source_target_pairs={{0,4},{4,8},{8,12},{12,16},{16,20},{20,24},{24,28},{28,0},{1,5},{5... | collective-permute-start | bytes 1376264 | tf_op jit(solution)/shard_map/ppermute | solution.py:201
  41.1 22.1 %collective-permute-start.7 = (bf16[64,3584]{1,0:T(8,128)(2,1)}, bf16[64,3584]{1,0:T(8,128)(2,1)}, u32[]{:S(2)}, u32[]{:S(2)}) collective-permute-start(bf16[64,3584]{1,0:T(8,128)(2,1)} %collective-permute-done.3.refs_1_), channel_id=1, source_target_pairs={{0,28},{4,0},{8,4},{12,8},{16,12},{20,16},{24,20},{28,24},{1,29},{... | collective-permute-start | bytes 1376264 | tf_op jit(solution)/shard_map/ppermute | solution.py:201
  50.5 16.8 %collective-permute-start.12 = (bf16[64,3584]{1,0:T(8,128)(2,1)}, bf16[64,3584]{1,0:T(8,128)(2,1)}, u32[]{:S(2)}, u32[]{:S(2)}) collective-permute-start(bf16[64,3584]{1,0:T(8,128)(2,1)} %collective-permute-done.9.refs_0_), channel_id=1, source_target_pairs={{0,28},{4,0},{8,4},{12,8},{16,12},{20,16},{24,20},{28,24},{1,29},{... | collective-permute-start | bytes 1376264 | tf_op jit(solution)/shard_map/ppermute | solution.py:201
  51.1 17.3 %collective-permute-start.13 = (bf16[64,3584]{1,0:T(8,128)(2,1)}, bf16[64,3584]{1,0:T(8,128)(2,1)}, u32[]{:S(2)}, u32[]{:S(2)}) collective-permute-start(bf16[64,3584]{1,0:T(8,128)(2,1)} %collective-permute-done.8.refs_1_), channel_id=1, source_target_pairs={{0,4},{4,8},{8,12},{12,16},{16,20},{20,24},{24,28},{28,0},{1,5},{5... | collective-permute-start | bytes 1376264 | tf_op jit(solution)/shard_map/ppermute | solution.py:201
  52.0 16.3 %copy-start.2 = (bf16[512,384]{1,0:T(8,128)(2,1)S(1)}, bf16[512,384]{1,0:T(8,128)(2,1)}, u32[]{:S(2)}) copy-start(bf16[512,384]{1,0:T(8,128)(2,1)} %fusion.1.refs_7_) | copy-start | bytes 1179652
  52.0 33.2 %all-to-all-start.1 = ((bf16[32,24,1024]{2,1,0:T(8,128)(2,1)}), bf16[32,24,1024]{2,1,0:T(8,128)(2,1)S(1)}, u32[]{:S(2)}, u32[]{:S(2)}) async-start(bf16[32,24,1024]{2,1,0:T(8,128)(2,1)} %bitcast.42), calls=%async_computation.1 | async-start | bytes 3145728 | tf_op jit(solution)/shard_map/all_to_all | solution.py:220
  63.1 15.0 %copy-start.4 = (bf16[512,128]{1,0:T(8,128)(2,1)S(1)}, bf16[512,128]{1,0:T(8,128)(2,1)}, u32[]{:S(2)}) copy-start(bf16[512,128]{1,0:T(8,128)(2,1)} %fusion.8.refs_3_) | copy-start | bytes 393220
  63.1 15.0 %collective-permute-start.10 = (bf16[64,3584]{1,0:T(8,128)(2,1)}, bf16[64,3584]{1,0:T(8,128)(2,1)S(1)}, u32[]{:S(2)}, u32[]{:S(2)}) collective-permute-start(bf16[64,3584]{1,0:T(8,128)(2,1)} %collective-permute-done.6.refs_2_), channel_id=1, source_target_pairs={{0,4},{4,8},{8,12},{12,16},{16,20},{20,24},{24,28},{28,0},{1,5},{5... | collective-permute-start | bytes 1376264 | tf_op jit(solution)/shard_map/ppermute | solution.py:201
  63.2 14.9 %collective-permute-start.11 = (bf16[64,3584]{1,0:T(8,128)(2,1)}, bf16[64,3584]{1,0:T(8,128)(2,1)S(1)}, u32[]{:S(2)}, u32[]{:S(2)}) collective-permute-start(bf16[64,3584]{1,0:T(8,128)(2,1)} %collective-permute-done.7.refs_3_), channel_id=1, source_target_pairs={{0,28},{4,0},{8,4},{12,8},{16,12},{20,16},{24,20},{28,24},{1,29},{... | collective-permute-start | bytes 1376264 | tf_op jit(solution)/shard_map/ppermute | solution.py:201
  85.2 23.7 %all-to-all-start.2 = ((bf16[32,16,1024]{2,1,0:T(8,128)(2,1)}), bf16[32,16,1024]{2,1,0:T(8,128)(2,1)}, u32[]{:S(2)}, u32[]{:S(2)}) async-start(bf16[32,16,1024]{2,1,0:T(8,128)(2,1)} %bitcast.43), calls=%async_computation.2 | async-start | bytes 2097152 | tf_op jit(solution)/shard_map/all_to_all | solution.py:220
  112.2 31.6 %copy-start.7 = (f32[1,1024]{1,0:T(1,128)S(1)}, f32[1,1024]{1,0:T(1,128)}, u32[]{:S(2)}) copy-start(f32[1,1024]{1,0:T(1,128)} %param.17) | copy-start | bytes 12292
  112.2 31.6 %copy-start.8 = (f32[1,1024]{1,0:T(1,128)S(1)}, f32[1,1024]{1,0:T(1,128)}, u32[]{:S(2)}) copy-start(f32[1,1024]{1,0:T(1,128)} %param.18) | copy-start | bytes 12292
  112.2 17.5 %all-to-all-start.3 = ((f32[64,1,384]{2,1,0:T(1,128)}), f32[64,1,384]{2,1,0:T(1,128)S(1)}, u32[]{:S(2)}, u32[]{:S(2)}) async-start(f32[64,1,384]{2,1,0:T(1,128)} %shard_map.105), calls=%async_computation.3 | async-start | bytes 196608 | tf_op jit(solution)/shard_map/all_to_all | solution.py:319
  (4 other events, 23.2 us)

commit v5 on v4

--- a/solution.py
+++ b/solution.py
@@ -175,6 +175,15 @@
     )(*operands)
 
 
+def terms_kernel(parts, query, eigen, terms):
+    cores = jnp.sum(parts[...], axis=0)
+    scaled = cores / eigen[...]
+    score = jnp.sum(query[...] * scaled, axis=1, keepdims=True)
+    own = jnp.sum(cores * scaled, axis=1, keepdims=True)
+    lane = lax.broadcasted_iota(jnp.int32, terms.shape, 1)
+    terms[...] = jnp.where(lane == 0, score, own)
+
+
 def per_device(
     hidden, down_weight, resid, target, gain, query_left, query_right, query_core, eigen, lengths
 ):
@@ -333,10 +342,12 @@
     token = seq * block_rows + tensor * strip + jnp.arange(strip, dtype=jnp.int32)
     member = ((token[None, :] >= starts[:, None]) & (token[None, :] < ends[:, None])).astype(F32)
     partial_cores = jnp.dot(member, outer, precision=lax.Precision.HIGHEST)
-    cores = jnp.sum(lax.all_to_all(partial_cores, ("seq", "tensor"), 0, 0, tiled=True), axis=0)
-    scaled = cores / eigen[0]
-    score, own_term = jnp.sum(query_core[0] * scaled), jnp.sum(cores * scaled)
-    terms = jnp.where(lax.broadcasted_iota(jnp.int32, (layers, 2), 1) == 0, score, own_term)
+    parts = lax.all_to_all(partial_cores, ("seq", "tensor"), 0, 0, tiled=True)
+    terms = pl.pallas_call(
+        terms_kernel,
+        out_shape=jax.ShapeDtypeStruct((layers, 2), F32),
+        compiler_params=pltpu.CompilerParams(vmem_limit_bytes=VMEM_BYTES),
+    )(parts.reshape(parts.shape[0], 1, rank * rank), query_core, eigen)
     terms = jnp.sum(lax.all_to_all(terms, "pipe", 0, 0, tiled=True), axis=0)
     return (terms[0] / jnp.sqrt(terms[1] + 1e-06)).reshape(1)
 

time: 158 us -> 156 us (0.987)
  other arithmetic: 6.81 us -> 4.91 us
where the time goes in v5:
time: 156 us
  starting transfers between devices  52.3 us (34%)
  Pallas kernels  33 us (21%)
  waiting for transfers between devices  32.9 us (21%)
  blocking collectives  22 us (14%)
  local copies, waits for them, and re-layouts  5.94 us (4%)
  other arithmetic  4.91 us (3%)
  between operations  2.35 us (2%)
  matrix products  2.23 us (1%)
    pallas_call x4, Pallas kernels, product(): pl.pallas_call(functools.partial(product_kernel, len(pieces), len(extra)...  28.4 us
    ppermute x7, starting transfers between devices, move(): lax.ppermute(pair[1], 'seq', down)  17.9 us
    all_to_all x2, starting transfers between devices, exchange(): lax.all_to_all(sent.reshape(peers, -1, width), ('tensor', 'pipe'), 0, 0)  17.4 us
    all_to_all x2, waiting for transfers between devices, exchange(): lax.all_to_all(sent.reshape(peers, -1, width), ('tensor', 'pipe'), 0, 0)  16.2 us
    all_to_all x1, blocking collectives, per_device(): parts = lax.all_to_all(partial_cores, ('seq', 'tensor'), 0, 0, tiled=True)  12.6 us
    all_to_all x1, waiting for transfers between devices, per_device(): packed = lax.all_to_all(packed, ('pipe', 'seq'), 0, 0)  9.46 us
    all_to_all x1, blocking collectives, per_device(): terms = jnp.sum(lax.all_to_all(terms, 'pipe', 0, 0, tiled=True), axis=0)  9.41 us
    all_to_all x1, starting transfers between devices, per_device(): packed = lax.all_to_all(packed, ('pipe', 'seq'), 0, 0)  7.68 us
  transfers between devices with their start and end apart: 18, of which 7 were waited for; matrix products, arithmetic and copies ran while one was open for 5% of the time, Pallas kernels for 19%

profile of v5, /device:TPU:1, one launch (start us, length us, event | category | flops | bytes accessed | tf_op | source)
XLA Modules:
  0.0 155.7 jit_solution(598771157351058896)
XLA Ops:
  0.0 2.2 %slice_bitcast_fusion = (bf16[64,3584]{1,0:T(8,128)(2,1)}, bf16[64,3584]{1,0:T(8,128)(2,1)}) fusion(bf16[1,128,3584]{2,1,0:T(8,128)(2,1)} %param.10), kind=kLoop, calls=%fused_computation.8 | loop fusion | bytes 1835008 | tf_op jit(solution)/shard_map/slice | solution.py:231
  2.2 2.5 %collective-permute-start = (bf16[64,3584]{1,0:T(8,128)(2,1)}, bf16[64,3584]{1,0:T(8,128)(2,1)}, u32[]{:S(2)}, u32[]{:S(2)}) collective-permute-start(bf16[64,3584]{1,0:T(8,128)(2,1)} %get-tuple-element.39), channel_id=1, source_target_pairs={{0,4},{4,8},{8,12},{12,16},{16,20},{20,24},{24,28},{28,0},{1,5},{5... | collective-permute-start | bytes 1376264 | tf_op jit(solution)/shard_map/ppermute | solution.py:210
  4.7 3.9 %collective-permute-start.1 = (bf16[64,3584]{1,0:T(8,128)(2,1)}, bf16[64,3584]{1,0:T(8,128)(2,1)}, u32[]{:S(2)}, u32[]{:S(2)}) collective-permute-start(bf16[64,3584]{1,0:T(8,128)(2,1)} %get-tuple-element.38), channel_id=1, source_target_pairs={{0,28},{4,0},{8,4},{12,8},{16,12},{20,16},{24,20},{28,24},{1,29},{... | collective-permute-start | bytes 1376264 | tf_op jit(solution)/shard_map/ppermute | solution.py:210
  9.8 2.7 %collective-permute-start.5 = (bf16[64,3584]{1,0:T(8,128)(2,1)}, bf16[64,3584]{1,0:T(8,128)(2,1)}, u32[]{:S(2)}, u32[]{:S(2)}) collective-permute-start(bf16[64,3584]{1,0:T(8,128)(2,1)} %get-tuple-element.39), channel_id=1, source_target_pairs={{0,28},{4,0},{8,4},{12,8},{16,12},{20,16},{24,20},{28,24},{1,29},{... | collective-permute-start | bytes 1376264 | tf_op jit(solution)/shard_map/ppermute | solution.py:210
  12.5 5.8 %all-to-all-start = ((f32[8,32,1024]{2,1,0:T(8,128)}), f32[8,32,1024]{2,1,0:T(8,128)S(1)}, u32[]{:S(2)}, u32[]{:S(2)}) async-start(f32[8,32,1024]{2,1,0:T(8,128)} %broadcast_in_dim.82), calls=%async_computation | async-start | bytes 2097152 | tf_op jit(solution)/shard_map/all_to_all | solution.py:238
  22.5 2.7 %collective-permute-start.3 = (bf16[64,3584]{1,0:T(8,128)(2,1)}, bf16[64,3584]{1,0:T(8,128)(2,1)}, u32[]{:S(2)}, u32[]{:S(2)}) collective-permute-start(bf16[64,3584]{1,0:T(8,128)(2,1)} %collective-permute-done.1.refs_2_), channel_id=1, source_target_pairs={{0,28},{4,0},{8,4},{12,8},{16,12},{20,16},{24,20},{28,24},{1,29},{... | collective-permute-start | bytes 1376264 | tf_op jit(solution)/shard_map/ppermute | solution.py:210
  25.7 3.4 %collective-permute-done.4.refs_4_ = bf16[64,3584]{1,0:T(8,128)(2,1)} collective-permute-done((bf16[64,3584]{1,0:T(8,128)(2,1)}, bf16[64,3584]{1,0:T(8,128)(2,1)}, u32[]{:S(2)}, u32[]{:S(2)}) %collective-permute-start.4) | collective-permute-done | bytes 458784 | tf_op jit(solution)/shard_map/ppermute | solution.py:210
  29.0 2.7 %collective-permute-start.9 = (bf16[64,3584]{1,0:T(8,128)(2,1)}, bf16[64,3584]{1,0:T(8,128)(2,1)}, u32[]{:S(2)}, u32[]{:S(2)}) collective-permute-start(bf16[64,3584]{1,0:T(8,128)(2,1)} %collective-permute-done.5.refs_3_), channel_id=1, source_target_pairs={{0,28},{4,0},{8,4},{12,8},{16,12},{20,16},{24,20},{28,24},{1,29},{... | collective-permute-start | bytes 1376264 | tf_op jit(solution)/shard_map/ppermute | solution.py:210
  31.7 9.2 %shard_map.100.refs_4_ = bf16[768,1024]{1,0:T(8,128)(2,1)} custom-call(bf16[128,3584]{1,0:T(8,128)(2,1)S(1)} %bitcast.36, bf16[64,3584]{1,0:T(8,128)(2,1)} %collective-permute-done.refs_1_, bf16[64,3584]{1,0:T(8,128)(2,1)} %collective-permute-done.1.refs_2_, bf16[64,3584]{1,0:T(8,128)(2,1)} %collective-permute-done.5.refs_3_, ...), custom_call_target="tpu_custom_call" | custom-call | flops 1150000000 | bytes 65536 | tf_op jit(solution)/shard_map/pallas_call | solution.py:92
  41.1 2.7 %collective-permute-start.7 = (bf16[64,3584]{1,0:T(8,128)(2,1)}, bf16[64,3584]{1,0:T(8,128)(2,1)}, u32[]{:S(2)}, u32[]{:S(2)}) collective-permute-start(bf16[64,3584]{1,0:T(8,128)(2,1)} %collective-permute-done.3.refs_1_), channel_id=1, source_target_pairs={{0,28},{4,0},{8,4},{12,8},{16,12},{20,16},{24,20},{28,24},{1,29},{... | collective-permute-start | bytes 1376264 | tf_op jit(solution)/shard_map/ppermute | solution.py:210
  44.7 5.8 %shard_map.101 = bf16[768,1024]{1,0:T(8,128)(2,1)} custom-call(bf16[64,3584]{1,0:T(8,128)(2,1)} %collective-permute-done.2.refs_0_, bf16[64,3584]{1,0:T(8,128)(2,1)} %collective-permute-done.3.refs_1_, bf16[3584,1024]{1,0:T(8,128)(2,1)} %bitcast.39, bf16[768,128]{1,0:T(8,128)(2,1)S(1)} %copy-done.3, bf16[768,1024]{1,0:T(8,128)(2,1)} %shard_map.100.refs_4_), custom_call_target="tpu_custom_call" | custom-call | flops 6899999744 | bytes 65536 | tf_op jit(solution)/shard_map/pallas_call | solution.py:92
  52.1 11.0 %all-to-all-start.1 = ((bf16[32,24,1024]{2,1,0:T(8,128)(2,1)}), bf16[32,24,1024]{2,1,0:T(8,128)(2,1)S(1)}, u32[]{:S(2)}, u32[]{:S(2)}) async-start(bf16[32,24,1024]{2,1,0:T(8,128)(2,1)} %bitcast.42), calls=%async_computation.1 | async-start | bytes 3145728 | tf_op jit(solution)/shard_map/all_to_all | solution.py:229
  63.2 2.7 %collective-permute-start.11 = (bf16[64,3584]{1,0:T(8,128)(2,1)}, bf16[64,3584]{1,0:T(8,128)(2,1)S(1)}, u32[]{:S(2)}, u32[]{:S(2)}) collective-permute-start(bf16[64,3584]{1,0:T(8,128)(2,1)} %collective-permute-done.7.refs_3_), channel_id=1, source_target_pairs={{0,28},{4,0},{8,4},{12,8},{16,12},{20,16},{24,20},{28,24},{1,29},{... | collective-permute-start | bytes 1376264 | tf_op jit(solution)/shard_map/ppermute | solution.py:210
  65.9 1.4 collective-permute-done.12.refs_4_
  68.4 8.4 %shard_map.102.refs_4_ = bf16[512,1024]{1,0:T(8,128)(2,1)} custom-call(bf16[64,3584]{1,0:T(8,128)(2,1)} %collective-permute-done.9.refs_0_, bf16[64,3584]{1,0:T(8,128)(2,1)} %collective-permute-done.8.refs_1_, bf16[64,3584]{1,0:T(8,128)(2,1)} %collective-permute-done.6.refs_2_, bf16[64,3584]{1,0:T(8,128)(2,1)} %collective-permute-done.7.refs_3_, ...), custom_call_target="tpu_custom_call" | custom-call | flops 6899999744 | bytes 65536 | tf_op jit(solution)/shard_map/pallas_call | solution.py:92
  78.1 5.1 %shard_map.103 = bf16[512,1024]{1,0:T(8,128)(2,1)} custom-call(bf16[64,3584]{1,0:T(8,128)(2,1)S(1)} %collective-permute-done.10.refs_0_, bf16[64,3584]{1,0:T(8,128)(2,1)S(1)} %collective-permute-done.11.refs_1_, bf16[3584,1024]{1,0:T(8,128)(2,1)} %bitcast.41, bf16[512,128]{1,0:T(8,128)(2,1)S(1)} %copy-done.4, bf16[512,1024]{1,0:T(8,128)(2,1)} %shard_map.102.refs_4_), custom_call_target="tpu_custom_call" | custom-call | flops 6899999744 | bytes 65536 | tf_op jit(solution)/shard_map/pallas_call | solution.py:92
  83.2 2.1 %all-to-all-done.1.got = bf16[32,24,1024]{2,1,0:T(8,128)(2,1)S(1)} async-done(((bf16[32,24,1024]{2,1,0:T(8,128)(2,1)}), bf16[32,24,1024]{2,1,0:T(8,128)(2,1)S(1)}, u32[]{:S(2)}, u32[]{:S(2)}) %all-to-all-start.1) | async-done | bytes 1572896 | tf_op jit(solution)/shard_map/all_to_all | solution.py:229
  85.3 6.4 %all-to-all-start.2 = ((bf16[32,16,1024]{2,1,0:T(8,128)(2,1)}), bf16[32,16,1024]{2,1,0:T(8,128)(2,1)}, u32[]{:S(2)}, u32[]{:S(2)}) async-start(bf16[32,16,1024]{2,1,0:T(8,128)(2,1)} %bitcast.43), calls=%async_computation.2 | async-start | bytes 2097152 | tf_op jit(solution)/shard_map/all_to_all | solution.py:229
  94.8 14.2 %all-to-all-done.2.got = bf16[32,16,1024]{2,1,0:T(8,128)(2,1)} async-done(((bf16[32,16,1024]{2,1,0:T(8,128)(2,1)}), bf16[32,16,1024]{2,1,0:T(8,128)(2,1)}, u32[]{:S(2)}, u32[]{:S(2)}) %all-to-all-start.2) | async-done | bytes 1048608 | tf_op jit(solution)/shard_map/all_to_all | solution.py:229
  109.0 3.3 %shard_map.105 = f32[64,1,384]{2,1,0:T(1,128)} custom-call(bf16[32,16,1024]{2,1,0:T(8,128)(2,1)} %all-to-all-done.2.got, f32[16,1024]{1,0:T(8,128)S(1)} %slice.75.resid, f32[16,1024]{1,0:T(8,128)S(1)} %slice.77.aim, f32[256,1024]{1,0:T(8,128)S(1)} %bitcast.35, f32[24,256]{1,0:T(8,128)S(1)} %get-tuple-element.65.first, ...), custom_call_target="tpu_custom_call" | custom-call | tf_op jit(solution)/shard_map/pallas_call | solution.py:171
  112.2 7.7 %all-to-all-start.3 = ((f32[64,1,384]{2,1,0:T(1,128)}), f32[64,1,384]{2,1,0:T(1,128)S(1)}, u32[]{:S(2)}, u32[]{:S(2)}) async-start(f32[64,1,384]{2,1,0:T(1,128)} %shard_map.105), calls=%async_computation.3 | async-start | bytes 196608 | tf_op jit(solution)/shard_map/all_to_all | solution.py:328
  120.2 9.5 %all-to-all-done.3 = f32[64,1,384]{2,1,0:T(1,128)S(1)} async-done(((f32[64,1,384]{2,1,0:T(1,128)}), f32[64,1,384]{2,1,0:T(1,128)S(1)}, u32[]{:S(2)}, u32[]{:S(2)}) %all-to-all-start.3) | async-done | bytes 98336 | tf_op jit(solution)/shard_map/all_to_all | solution.py:328
  131.0 12.6 %all_to_all.38.parts = f32[32,1,1024]{2,1,0:T(1,128)S(1)} all-to-all(f32[32,1,1024]{2,1,0:T(1,128)S(1)} %all_to_all.28), channel_id=1, replica_groups=mesh['pipe'=8,'seq'=8,'tensor'=4] {'seq','tensor'}, dimensions={0} | all-to-all | bytes 262144 | tf_op jit(solution)/shard_map/all_to_all | solution.py:345
  143.8 9.4 %all_to_all.39 = f32[8,1,2]{2,1,0:T(1,128)S(1)} all-to-all(f32[8,1,2]{2,1,0:T(1,128)S(1)} %bitcast.37), channel_id=1, replica_groups=mesh['pipe'=8,'seq'=8,'tensor'=4] {'pipe'}, dimensions={0} | all-to-all | bytes 128 | tf_op jit(solution)/shard_map/all_to_all | solution.py:351
  (92 shorter events, 16.3 us)
Async XLA Ops:
  0.0 25.2 %copy-start = (bf16[1,3584,32]{1,2,0:T(8,128)(2,1)S(1)}, bf16[1,3584,32]{1,2,0:T(8,128)(2,1)}, u32[]{:S(2)}) copy-start(bf16[1,3584,32]{1,2,0:T(8,128)(2,1)} %param.16) | copy-start | bytes 688132
  0.0 8.7 %copy-start.7 = (f32[1,1024,32]{1,2,0:T(8,128)S(1)}, f32[1,1024,32]{1,2,0:T(8,128)}, u32[]{:S(2)}) copy-start(f32[1,1024,32]{1,2,0:T(8,128)} %param.15) | copy-start | bytes 393220
  2.2 20.2 %collective-permute-start = (bf16[64,3584]{1,0:T(8,128)(2,1)}, bf16[64,3584]{1,0:T(8,128)(2,1)}, u32[]{:S(2)}, u32[]{:S(2)}) collective-permute-start(bf16[64,3584]{1,0:T(8,128)(2,1)} %get-tuple-element.39), channel_id=1, source_target_pairs={{0,4},{4,8},{8,12},{12,16},{16,20},{20,24},{24,28},{28,0},{1,5},{5... | collective-permute-start | bytes 1376264 | tf_op jit(solution)/shard_map/ppermute | solution.py:210
  4.7 17.8 %collective-permute-start.1 = (bf16[64,3584]{1,0:T(8,128)(2,1)}, bf16[64,3584]{1,0:T(8,128)(2,1)}, u32[]{:S(2)}, u32[]{:S(2)}) collective-permute-start(bf16[64,3584]{1,0:T(8,128)(2,1)} %get-tuple-element.38), channel_id=1, source_target_pairs={{0,28},{4,0},{8,4},{12,8},{16,12},{20,16},{24,20},{28,24},{1,29},{... | collective-permute-start | bytes 1376264 | tf_op jit(solution)/shard_map/ppermute | solution.py:210
  9.8 19.3 %collective-permute-start.4 = (bf16[64,3584]{1,0:T(8,128)(2,1)}, bf16[64,3584]{1,0:T(8,128)(2,1)}, u32[]{:S(2)}, u32[]{:S(2)}) collective-permute-start(bf16[64,3584]{1,0:T(8,128)(2,1)} %get-tuple-element.38), channel_id=1, source_target_pairs={{0,4},{4,8},{8,12},{12,16},{16,20},{20,24},{24,28},{28,0},{1,5},{5... | collective-permute-start | bytes 1376264 | tf_op jit(solution)/shard_map/ppermute | solution.py:210
  9.8 19.3 %collective-permute-start.5 = (bf16[64,3584]{1,0:T(8,128)(2,1)}, bf16[64,3584]{1,0:T(8,128)(2,1)}, u32[]{:S(2)}, u32[]{:S(2)}) collective-permute-start(bf16[64,3584]{1,0:T(8,128)(2,1)} %get-tuple-element.39), channel_id=1, source_target_pairs={{0,28},{4,0},{8,4},{12,8},{16,12},{20,16},{24,20},{28,24},{1,29},{... | collective-permute-start | bytes 1376264 | tf_op jit(solution)/shard_map/ppermute | solution.py:210
  12.5 28.5 %all-to-all-start = ((f32[8,32,1024]{2,1,0:T(8,128)}), f32[8,32,1024]{2,1,0:T(8,128)S(1)}, u32[]{:S(2)}, u32[]{:S(2)}) async-start(f32[8,32,1024]{2,1,0:T(8,128)} %broadcast_in_dim.82), calls=%async_computation | async-start | bytes 2097152 | tf_op jit(solution)/shard_map/all_to_all | solution.py:238
  22.5 18.5 %collective-permute-start.2 = (bf16[64,3584]{1,0:T(8,128)(2,1)}, bf16[64,3584]{1,0:T(8,128)(2,1)}, u32[]{:S(2)}, u32[]{:S(2)}) collective-permute-start(bf16[64,3584]{1,0:T(8,128)(2,1)} %collective-permute-done.refs_1_), channel_id=1, source_target_pairs={{0,4},{4,8},{8,12},{12,16},{16,20},{20,24},{24,28},{28,0},{1,5},{5... | collective-permute-start | bytes 1376264 | tf_op jit(solution)/shard_map/ppermute | solution.py:210
  22.5 18.5 %collective-permute-start.3 = (bf16[64,3584]{1,0:T(8,128)(2,1)}, bf16[64,3584]{1,0:T(8,128)(2,1)}, u32[]{:S(2)}, u32[]{:S(2)}) collective-permute-start(bf16[64,3584]{1,0:T(8,128)(2,1)} %collective-permute-done.1.refs_2_), channel_id=1, source_target_pairs={{0,28},{4,0},{8,4},{12,8},{16,12},{20,16},{24,20},{28,24},{1,29},{... | collective-permute-start | bytes 1376264 | tf_op jit(solution)/shard_map/ppermute | solution.py:210
  29.0 21.4 %collective-permute-start.8 = (bf16[64,3584]{1,0:T(8,128)(2,1)}, bf16[64,3584]{1,0:T(8,128)(2,1)}, u32[]{:S(2)}, u32[]{:S(2)}) collective-permute-start(bf16[64,3584]{1,0:T(8,128)(2,1)} %collective-permute-done.4.refs_4_), channel_id=1, source_target_pairs={{0,4},{4,8},{8,12},{12,16},{16,20},{20,24},{24,28},{28,0},{1,5},{5... | collective-permute-start | bytes 1376264 | tf_op jit(solution)/shard_map/ppermute | solution.py:210
  29.0 21.4 %collective-permute-start.9 = (bf16[64,3584]{1,0:T(8,128)(2,1)}, bf16[64,3584]{1,0:T(8,128)(2,1)}, u32[]{:S(2)}, u32[]{:S(2)}) collective-permute-start(bf16[64,3584]{1,0:T(8,128)(2,1)} %collective-permute-done.5.refs_3_), channel_id=1, source_target_pairs={{0,28},{4,0},{8,4},{12,8},{16,12},{20,16},{24,20},{28,24},{1,29},{... | collective-permute-start | bytes 1376264 | tf_op jit(solution)/shard_map/ppermute | solution.py:210
  41.0 22.1 %collective-permute-start.6 = (bf16[64,3584]{1,0:T(8,128)(2,1)}, bf16[64,3584]{1,0:T(8,128)(2,1)}, u32[]{:S(2)}, u32[]{:S(2)}) collective-permute-start(bf16[64,3584]{1,0:T(8,128)(2,1)} %collective-permute-done.2.refs_0_), channel_id=1, source_target_pairs={{0,4},{4,8},{8,12},{12,16},{16,20},{20,24},{24,28},{28,0},{1,5},{5... | collective-permute-start | bytes 1376264 | tf_op jit(solution)/shard_map/ppermute | solution.py:210
  41.1 22.1 %collective-permute-start.7 = (bf16[64,3584]{1,0:T(8,128)(2,1)}, bf16[64,3584]{1,0:T(8,128)(2,1)}, u32[]{:S(2)}, u32[]{:S(2)}) collective-permute-start(bf16[64,3584]{1,0:T(8,128)(2,1)} %collective-permute-done.3.refs_1_), channel_id=1, source_target_pairs={{0,28},{4,0},{8,4},{12,8},{16,12},{20,16},{24,20},{28,24},{1,29},{... | collective-permute-start | bytes 1376264 | tf_op jit(solution)/shard_map/ppermute | solution.py:210
  50.5 16.8 %collective-permute-start.12 = (bf16[64,3584]{1,0:T(8,128)(2,1)}, bf16[64,3584]{1,0:T(8,128)(2,1)}, u32[]{:S(2)}, u32[]{:S(2)}) collective-permute-start(bf16[64,3584]{1,0:T(8,128)(2,1)} %collective-permute-done.9.refs_0_), channel_id=1, source_target_pairs={{0,28},{4,0},{8,4},{12,8},{16,12},{20,16},{24,20},{28,24},{1,29},{... | collective-permute-start | bytes 1376264 | tf_op jit(solution)/shard_map/ppermute | solution.py:210
  51.1 17.3 %collective-permute-start.13 = (bf16[64,3584]{1,0:T(8,128)(2,1)}, bf16[64,3584]{1,0:T(8,128)(2,1)}, u32[]{:S(2)}, u32[]{:S(2)}) collective-permute-start(bf16[64,3584]{1,0:T(8,128)(2,1)} %collective-permute-done.8.refs_1_), channel_id=1, source_target_pairs={{0,4},{4,8},{8,12},{12,16},{16,20},{20,24},{24,28},{28,0},{1,5},{5... | collective-permute-start | bytes 1376264 | tf_op jit(solution)/shard_map/ppermute | solution.py:210
  52.1 16.3 %copy-start.2 = (bf16[512,384]{1,0:T(8,128)(2,1)S(1)}, bf16[512,384]{1,0:T(8,128)(2,1)}, u32[]{:S(2)}) copy-start(bf16[512,384]{1,0:T(8,128)(2,1)} %fusion.1.refs_7_) | copy-start | bytes 1179652
  52.1 33.2 %all-to-all-start.1 = ((bf16[32,24,1024]{2,1,0:T(8,128)(2,1)}), bf16[32,24,1024]{2,1,0:T(8,128)(2,1)S(1)}, u32[]{:S(2)}, u32[]{:S(2)}) async-start(bf16[32,24,1024]{2,1,0:T(8,128)(2,1)} %bitcast.42), calls=%async_computation.1 | async-start | bytes 3145728 | tf_op jit(solution)/shard_map/all_to_all | solution.py:229
  63.1 15.0 %copy-start.4 = (bf16[512,128]{1,0:T(8,128)(2,1)S(1)}, bf16[512,128]{1,0:T(8,128)(2,1)}, u32[]{:S(2)}) copy-start(bf16[512,128]{1,0:T(8,128)(2,1)} %fusion.8.refs_3_) | copy-start | bytes 393220
  63.1 15.0 %collective-permute-start.10 = (bf16[64,3584]{1,0:T(8,128)(2,1)}, bf16[64,3584]{1,0:T(8,128)(2,1)S(1)}, u32[]{:S(2)}, u32[]{:S(2)}) collective-permute-start(bf16[64,3584]{1,0:T(8,128)(2,1)} %collective-permute-done.6.refs_2_), channel_id=1, source_target_pairs={{0,4},{4,8},{8,12},{12,16},{16,20},{20,24},{24,28},{28,0},{1,5},{5... | collective-permute-start | bytes 1376264 | tf_op jit(solution)/shard_map/ppermute | solution.py:210
  63.2 14.9 %collective-permute-start.11 = (bf16[64,3584]{1,0:T(8,128)(2,1)}, bf16[64,3584]{1,0:T(8,128)(2,1)S(1)}, u32[]{:S(2)}, u32[]{:S(2)}) collective-permute-start(bf16[64,3584]{1,0:T(8,128)(2,1)} %collective-permute-done.7.refs_3_), channel_id=1, source_target_pairs={{0,28},{4,0},{8,4},{12,8},{16,12},{20,16},{24,20},{28,24},{1,29},{... | collective-permute-start | bytes 1376264 | tf_op jit(solution)/shard_map/ppermute | solution.py:210
  85.3 23.7 %all-to-all-start.2 = ((bf16[32,16,1024]{2,1,0:T(8,128)(2,1)}), bf16[32,16,1024]{2,1,0:T(8,128)(2,1)}, u32[]{:S(2)}, u32[]{:S(2)}) async-start(bf16[32,16,1024]{2,1,0:T(8,128)(2,1)} %bitcast.43), calls=%async_computation.2 | async-start | bytes 2097152 | tf_op jit(solution)/shard_map/all_to_all | solution.py:229
  112.2 31.4 %copy-start.5 = (f32[1,1024]{1,0:T(1,128)S(1)}, f32[1,1024]{1,0:T(1,128)}, u32[]{:S(2)}) copy-start(f32[1,1024]{1,0:T(1,128)} %query.1) | copy-start | bytes 12292
  112.2 31.4 %copy-start.6 = (f32[1,1024]{1,0:T(1,128)S(1)}, f32[1,1024]{1,0:T(1,128)}, u32[]{:S(2)}) copy-start(f32[1,1024]{1,0:T(1,128)} %eigen.1) | copy-start | bytes 12292
  112.2 17.4 %all-to-all-start.3 = ((f32[64,1,384]{2,1,0:T(1,128)}), f32[64,1,384]{2,1,0:T(1,128)S(1)}, u32[]{:S(2)}, u32[]{:S(2)}) async-start(f32[64,1,384]{2,1,0:T(1,128)} %shard_map.105), calls=%async_computation.3 | async-start | bytes 196608 | tf_op jit(solution)/shard_map/all_to_all | solution.py:328
  (4 other events, 23.2 us)
